TPU v7x, 256 devices: a whole 4x4x8 slice. The times are simulated.
256 devices in a mesh: pb: 8 (over x, core), ka: 32 (over z, y).
Axes of the slice: x: 4, y: 4, z: 8, core: 2. Of those that a mesh axis runs over, the one named last changes fastest.
Arguments:
- queries: bfloat16 [32768, 512], P(('pb', 'ka')), may hold values from -9 to 9
- keys: bfloat16 [32768, 512], P(('ka', 'pb')), may hold values from -6 to 6
- values: bfloat16 [32768, 512], P(('ka', 'pb')), may hold values from -6 to 6
- block_pairs: int32 [6400, 2], replicated, may hold values from 0 to 255, as said below
- doc_lengths: int32 [16], replicated, may hold values from 1 to 8192, 32768 in all
Outputs:
- attended: bfloat16 [32768, 512], P(('pb', 'ka'))
Inputs may be any that keep to these rules, and one draw needn't show every extreme that they name: `block_pairs`: each row is (query block, key block) with the key block at most the query block; rows come grouped by query block, 25 rows each, and the first row of each group is the block with itself; a pair may appear more than once.
All inputs are finite; a program needn't handle non-finite values.
Results may differ from a plain program's by a relative error of at most 0.02.
Values may be sent and summed in bfloat16 or wider, within the bound.
No kernel may reach another device: no remote copies, remote signals or barrier semaphores. Data moves between devices by JAX's collectives and lax.ppermute only.
A program may use at most 64 MiB of HBM per device.

v0:
```python
import functools
import math

import jax
import jax.numpy as jnp
from jax import lax
from jax.experimental import pallas as pl
from jax.experimental.pallas import tpu as pltpu
from jax.sharding import Mesh
from jax.sharding import PartitionSpec as P

H = 4
DH = 128
BLK = 128
NX, NC, NZ, NY = 4, 2, 8, 4
PLANE = 32
NQ = NX * NY
PLANES = 3
NK = PLANES * NY * NC
STAT_ROWS = 16
ROWS = DH + STAT_ROWS
UNROLL = 8
COUNT_AT = NQ * NK // 2 + UNROLL
QUERY_AT = COUNT_AT + 1
KEY_AT = QUERY_AT + NQ
PLAN = KEY_AT + NK + 1
NOWHERE = 1 << 20
NEG = -1e30
SCALE = math.log2(math.e) / math.sqrt(DH)


def device(x, c, z, y):
    return ((x * NC + c) * NZ + z) * NY + y


PLACE = [
    [7, 3, 4, 0, 5, 6, 2, 1],
    [3, 5, 1, 2, 6, 0, 7, 4],
    [1, 6, 2, 5, 0, 3, 4, 7],
    [2, 7, 4, 6, 0, 5, 3, 1],
    [6, 2, 0, 5, 3, 7, 4, 1],
    [5, 4, 2, 0, 6, 1, 7, 3],
    [1, 6, 0, 7, 2, 4, 3, 5],
    [1, 7, 5, 3, 0, 6, 4, 2],
]
LIVES = [
    [
        sum(PLACE[(z + 1) % NZ].index(2 * x + c) << (3 * z) for z in range(NZ))
        for c in range(NC)
    ]
    for x in range(NX)
]


def transpose_pairs(back):
    pairs = []
    for x in range(NX):
        for c in range(NC):
            for z in range(NZ):
                for y in range(NY):
                    p = 2 * x + c
                    home = device(x, c, z, y)
                    work = device(PLACE[p][z] // 2, PLACE[p][z] % 2, (p - 1) % NZ, y)
                    pairs.append((work, home) if back else (home, work))
    return pairs


def ring(n, d):
    return [(i, (i + d) % n) for i in range(n)]


def pack_queries_kernel(q_ref, out_ref):
    for h in range(H):
        part = q_ref[:, h * DH : (h + 1) * DH].astype(jnp.float32).T.astype(jnp.bfloat16)
        for x in range(NX):
            out_ref[x * H + h] = part


def pack_keys_kernel(y_ref, k_ref, v_ref, *out_refs):
    for d, out_ref in enumerate(out_refs):
        at = pl.ds(pl.multiple_of(lax.rem(y_ref[0] + d, H) * DH, DH), DH)
        out_ref[0] = k_ref[:, at]
        out_ref[1] = v_ref[:, at].astype(jnp.float32).T.astype(jnp.bfloat16)


def join_kernel(*refs):
    at = 0
    for ref in refs[:-1]:
        refs[-1][at : at + ref.shape[0]] = ref[...]
        at += ref.shape[0]


def join(parts):
    count = sum(p.shape[0] for p in parts)
    return pl.pallas_call(
        join_kernel,
        out_shape=jax.ShapeDtypeStruct((count,) + parts[0].shape[1:], parts[0].dtype),
        in_specs=[VMEM] * len(parts),
        out_specs=VMEM,
        compiler_params=SMALL,
        cost_estimate=LIGHT,
    )(*parts)


def lowest_bit(mask):
    return 31 - lax.clz(mask & -mask)


def plan_kernel(need_ref, qblk_ref, kblk_ref, plan_ref):
    def list_row(j, count):
        plan_ref[QUERY_AT + j] = qblk_ref[j]

        def entry(carry):
            mask, count = carry
            rest = mask & (mask - 1)
            second = jnp.where(rest == 0, NK, lowest_bit(rest))
            plan_ref[count] = j * 1024 + lowest_bit(mask) * 32 + second
            return rest & (rest - 1), count + 1

        return lax.while_loop(lambda c: c[0] != 0, entry, (need_ref[j], count))[1]

    count = lax.fori_loop(0, NQ, list_row, jnp.int32(0))
    for u in range(UNROLL):
        plan_ref[count + u] = NQ * 1024 + NK * 32 + NK
    plan_ref[COUNT_AT] = count
    for s in range(NK):
        plan_ref[KEY_AT + s] = kblk_ref[s]
    plan_ref[KEY_AT + NK] = NOWHERE


def attend_kernel(plan_ref, start_ref, q_ref, kv_ref, out_ref, acc, top, total):
    acc[...] = jnp.zeros_like(acc)
    top[...] = jnp.full_like(top, NEG)
    total[...] = jnp.zeros_like(total)
    key_row = lax.broadcasted_iota(jnp.int32, (BLK, BLK), 0)
    lane = lax.broadcasted_iota(jnp.int32, (1, BLK), 1)

    def step(i, carry):
        done = []
        for u in range(UNROLL):
            entry = plan_ref[i * UNROLL + u]
            j = lax.shift_right_logical(entry, 10)
            jq = jnp.minimum(j, NQ - 1)
            slots = (lax.shift_right_logical(entry, 5) & 31, entry & 31)
            held = [jnp.minimum(s, NK - 1) for s in slots]
            scores = jnp.dot(
                jnp.concatenate([kv_ref[s, 0] for s in held], axis=0),
                q_ref[jq],
                preferred_element_type=jnp.float32,
            )
            masked = []
            for n, s in enumerate(slots):
                base = plan_ref[KEY_AT + s] * BLK
                low = start_ref[pl.ds(jq, 1), :] - base
                high = plan_ref[QUERY_AT + jq] * BLK + lane - base
                allowed = (key_row >= low) & (key_row <= high)
                part = scores[n * BLK : (n + 1) * BLK]
                masked.append(jnp.where(allowed, part * SCALE, NEG))
            scores = jnp.concatenate(masked, axis=0)
            peak = jnp.max(scores, axis=0, keepdims=True)
            weights = jnp.exp2(scores - peak)
            mass = jnp.sum(weights, axis=0, keepdims=True)
            part = jnp.dot(
                jnp.concatenate([kv_ref[s, 1] for s in held], axis=1),
                weights.astype(jnp.bfloat16),
                preferred_element_type=jnp.float32,
            )
            done.append((j, peak, mass, part))
        for j, peak, mass, part in done:
            at = pl.ds(j, 1)
            old = top[at, :]
            new = jnp.maximum(old, peak)
            keep = jnp.exp2(old - new)
            gain = jnp.exp2(peak - new)
            top[at, :] = new
            total[at, :] = total[at, :] * keep + mass * gain
            acc[j] = acc[j] * keep + part * gain
        return carry

    lax.fori_loop(0, (plan_ref[COUNT_AT] + UNROLL - 1) // UNROLL, step, 0)

    mass = total[:NQ, :]
    some = mass > 0.0
    safe = jnp.where(some, mass, 1.0)
    inverse = 1.0 / safe
    level = jnp.where(some, top[:NQ, :] + jnp.log2(safe), NEG)
    first = level.astype(jnp.bfloat16).astype(jnp.float32)
    second = (level - first).astype(jnp.bfloat16).astype(jnp.float32)
    third = level - first - second
    row = lax.broadcasted_iota(jnp.int32, (STAT_ROWS, BLK), 0)
    for j in range(NQ):
        one = slice(j, j + 1)
        out_ref[j, :DH, :] = (acc[j] * inverse[one]).astype(jnp.bfloat16)
        stat = jnp.where(
            row == 0, first[one], jnp.where(row == 1, second[one], third[one])
        )
        out_ref[j, DH:, :] = jnp.where(row < 3, stat, 0.0).astype(jnp.bfloat16)


def combine_kernel(parts_ref, out_ref):
    for h in range(H):
        levels = []
        for r in range(NX):
            stat = parts_ref[r * H + h, DH:, :].astype(jnp.float32)
            levels.append(stat[0:1] + stat[1:2] + stat[2:3])
        peak = functools.reduce(jnp.maximum, levels)
        shares = [jnp.exp2(level - peak) for level in levels]
        inverse = 1.0 / functools.reduce(jnp.add, shares)
        value = functools.reduce(
            jnp.add,
            [
                parts_ref[r * H + h, :DH, :].astype(jnp.float32) * (shares[r] * inverse)
                for r in range(NX)
            ],
        )
        out_ref[:, h * DH : (h + 1) * DH] = value.T.astype(jnp.bfloat16)


VMEM = pl.BlockSpec(memory_space=pltpu.VMEM)
SMEM = pl.BlockSpec(memory_space=pltpu.SMEM)
LIGHT = pl.CostEstimate(flops=1024, bytes_accessed=1024, transcendentals=0)
SMALL = pltpu.CompilerParams(vmem_limit_bytes=8 << 20)


def on_device(queries, keys, values, block_pairs, doc_lengths):
    x, c, z, y = (lax.axis_index(name) for name in ("x", "c", "z", "y"))
    bf16 = jnp.bfloat16

    piece = jax.ShapeDtypeStruct((2, BLK, DH), bf16)
    split = pl.pallas_call(
        pack_keys_kernel,
        out_shape=[piece] * NY,
        in_specs=[SMEM, VMEM, VMEM],
        out_specs=[VMEM] * NY,
        compiler_params=pltpu.CompilerParams(vmem_limit_bytes=63 << 20),
        cost_estimate=LIGHT,
    )(y.reshape(1), keys, values)
    moved = lax.ppermute(queries, ("x", "c", "z", "y"), transpose_pairs(False))
    pieces = [split[0]] + [lax.ppermute(split[d], "y", ring(NY, d)) for d in range(1, NY)]

    spread = pl.pallas_call(
        pack_queries_kernel,
        out_shape=jax.ShapeDtypeStruct((NQ, DH, BLK), bf16),
        in_specs=[VMEM],
        out_specs=VMEM,
        compiler_params=SMALL,
        cost_estimate=LIGHT,
    )(moved)
    spread, *pieces = lax.optimization_barrier((spread, *pieces))
    mine = lax.all_to_all(spread, ("x", "y"), 0, 0, tiled=True)

    here = jnp.stack(pieces)
    near = [here, lax.ppermute(here, "z", ring(NZ, 1)), lax.ppermute(here, "z", ring(NZ, -1))]
    near[0], near[1], block_pairs, doc_lengths, x, c, z, y = lax.optimization_barrier(
        (near[0], near[1], block_pairs, doc_lengths, x, c, z, y)
    )
    other = [lax.ppermute(b, "c", ring(NC, 1)) for b in near]

    slot = jnp.arange(NQ, dtype=jnp.int32)
    digits = [
        lax.shift_right_logical(jnp.where(c == 0, LIVES[n][0], LIVES[n][1]), 3 * z) & 7
        for n in range(NX)
    ]
    lives = functools.reduce(
        lambda rest, n: jnp.where(slot // NY == n, digits[n], rest), range(NX), slot
    )
    query_block = PLANE * lax.rem(z + 1, NZ) + NY * lives + slot % NY
    slot = jnp.arange(NK, dtype=jnp.int32)
    group = (slot // NY) % PLANES
    plane = lax.rem(z + jnp.where(group == 0, 0, jnp.where(group == 1, NZ - 1, 1)), NZ)
    row = lax.rem(y + NY - slot % NY, NY)
    core = jnp.where(slot < PLANES * NY, c, 1 - c)
    key_block = PLANE * plane + 8 * row + 2 * x + core
    ends = jnp.sum(
        jnp.where(
            jnp.arange(16)[:, None] <= jnp.arange(16)[None, :], doc_lengths[:, None], 0
        ),
        axis=0,
    )
    token = query_block[:, None] * BLK + jnp.arange(BLK, dtype=jnp.int32)[None, :]
    start = jnp.max(jnp.where(ends[:, None, None] <= token[None], ends[:, None, None], 0), axis=0)
    first = jnp.max(
        jnp.where(ends[:, None] <= query_block[None] * BLK, ends[:, None], 0), axis=0
    )
    hit_query = (block_pairs[:, 0][None, :] == query_block[:, None]).astype(bf16)
    hit_key = (block_pairs[:, 1][None, :] == key_block[:, None]).astype(bf16)
    listed = lax.dot_general(
        hit_query, hit_key, (((1,), (1,)), ((), ())), preferred_element_type=jnp.float32
    )
    need = (
        (listed > 0.5)
        & (key_block[None, :] * BLK + (BLK - 1) >= first[:, None])
        & (key_block[None, :] <= query_block[:, None])
    )
    bits = jnp.left_shift(jnp.int32(1), jnp.arange(NK, dtype=jnp.int32))
    need = jnp.sum(jnp.where(need, bits[None, :], 0), axis=1)

    plan = pl.pallas_call(
        plan_kernel,
        out_shape=jax.ShapeDtypeStruct((PLAN,), jnp.int32),
        in_specs=[SMEM] * 3,
        out_specs=SMEM,
        compiler_params=SMALL,
        cost_estimate=LIGHT,
    )(need, query_block, key_block)
    parts = pl.pallas_call(
        attend_kernel,
        out_shape=jax.ShapeDtypeStruct((NQ, ROWS, BLK), bf16),
        in_specs=[SMEM, VMEM, VMEM, VMEM],
        out_specs=VMEM,
        scratch_shapes=[
            pltpu.VMEM((NQ + 1, DH, BLK), jnp.float32),
            pltpu.VMEM((NQ + 8, BLK), jnp.float32),
            pltpu.VMEM((NQ + 8, BLK), jnp.float32),
        ],
        compiler_params=pltpu.CompilerParams(vmem_limit_bytes=24 << 20),
    )(plan, start, mine, join([*near, *other]))

    gathered = lax.all_to_all(parts, ("x", "y"), 0, 0, tiled=True)
    result = pl.pallas_call(
        combine_kernel,
        out_shape=jax.ShapeDtypeStruct((BLK, H * DH), bf16),
        in_specs=[VMEM],
        out_specs=VMEM,
        compiler_params=SMALL,
        cost_estimate=LIGHT,
    )(gathered)
    return lax.ppermute(result, ("x", "c", "z", "y"), transpose_pairs(True))


def solution(mesh):
    fine = Mesh(mesh.devices.reshape(NX, NC, NZ, NY), ("x", "c", "z", "y"))
    return jax.shard_map(
        on_device,
        mesh=fine,
        in_specs=(
            P(("x", "c", "z", "y"), None),
            P(("z", "y", "x", "c"), None),
            P(("z", "y", "x", "c"), None),
            P(),
            P(),
        ),
        out_specs=P(("x", "c", "z", "y"), None),
        check_vma=False,
    )
```

profile of v0, /device:TPU:6, one launch (start us, length us, event | category | flops | bytes accessed | tf_op | source)
XLA Modules:
  0.0 64.0 jit_solution(15696356450956495127)
XLA Ops:
  0.0 0.0 copy-start
  0.0 0.0 copy-start.1
  0.0 6.1 %collective-permute-start = (bf16[128,512]{1,0:T(8,128)(2,1)}, bf16[128,512]{1,0:T(8,128)(2,1)S(1)}, u32[]{:S(2)}, u32[]{:S(2)}) collective-permute-start(bf16[128,512]{1,0:T(8,128)(2,1)} %param.5), channel_id=1, source_target_pairs={{0,252},{1,253},{2,254},{3,255},{4,124},{5,125},{6,126},{7,127},{8... | collective-permute-start | bytes 393224 | tf_op jit(solution)/shard_map/ppermute | solution.py:238
  6.1 1.8 %shard_map.56 = (bf16[2,128,128]{2,1,0:T(8,128)(2,1)}, bf16[2,128,128]{2,1,0:T(8,128)(2,1)}, bf16[2,128,128]{2,1,0:T(8,128)(2,1)}, bf16[2,128,128]{2,1,0:T(8,128)(2,1)}) custom-call(s32[1]{0:T(128)} %bitcast.y_ref, bf16[128,512]{1,0:T(8,128)(2,1)} %k_ref.1, bf16[128,512]{1,0:T(8,128)(2,1)} %v_ref.1), custom_call_target="tpu_custom_call" | custom-call | flops 1024 | bytes 1024 | tf_op jit(solution)/shard_map/pallas_call | solution.py:230
  7.9 1.6 %collective-permute-start.1 = (bf16[2,128,128]{2,1,0:T(8,128)(2,1)}, bf16[2,128,128]{2,1,0:T(8,128)(2,1)S(1)}, u32[]{:S(2)}, u32[]{:S(2)}) collective-permute-start(bf16[2,128,128]{2,1,0:T(8,128)(2,1)} %get-tuple-element.23), channel_id=1, source_target_pairs={{0,1},{1,2},{2,3},{3,0},{4,5},{5,6},{6,7},{7,4},{8,9},{9,10},{10,1... | collective-permute-start | bytes 196616 | tf_op jit(solution)/shard_map/ppermute | solution.py:239
  9.5 2.9 %collective-permute-start.2 = (bf16[2,128,128]{2,1,0:T(8,128)(2,1)}, bf16[2,128,128]{2,1,0:T(8,128)(2,1)S(1)}, u32[]{:S(2)}, u32[]{:S(2)}) collective-permute-start(bf16[2,128,128]{2,1,0:T(8,128)(2,1)} %get-tuple-element.24), channel_id=1, source_target_pairs={{0,2},{1,3},{2,0},{3,1},{4,6},{5,7},{6,4},{7,5},{8,10},{9,11},{10,... | collective-permute-start | bytes 196616 | tf_op jit(solution)/shard_map/ppermute | solution.py:239
  12.4 1.3 %collective-permute-start.3 = (bf16[2,128,128]{2,1,0:T(8,128)(2,1)}, bf16[2,128,128]{2,1,0:T(8,128)(2,1)S(1)}, u32[]{:S(2)}, u32[]{:S(2)}) collective-permute-start(bf16[2,128,128]{2,1,0:T(8,128)(2,1)} %get-tuple-element.25), channel_id=1, source_target_pairs={{0,3},{1,0},{2,1},{3,2},{4,7},{5,4},{6,5},{7,6},{8,11},{9,8},{10,9... | collective-permute-start | bytes 196616 | tf_op jit(solution)/shard_map/ppermute | solution.py:239
  13.7 0.0 collective-permute-done.q_ref
  13.7 0.9 %shard_map.55 = bf16[16,128,128]{2,1,0:T(8,128)(2,1)} custom-call(bf16[128,512]{1,0:T(8,128)(2,1)S(1)} %collective-permute-done.q_ref), custom_call_target="tpu_custom_call" | custom-call | flops 1024 | bytes 1024 | tf_op jit(solution)/shard_map/pallas_call | solution.py:241
  14.6 0.0 collective-permute-done.1
  14.6 1.0 %collective-permute-done.2 = bf16[2,128,128]{2,1,0:T(8,128)(2,1)S(1)} collective-permute-done((bf16[2,128,128]{2,1,0:T(8,128)(2,1)}, bf16[2,128,128]{2,1,0:T(8,128)(2,1)S(1)}, u32[]{:S(2)}, u32[]{:S(2)}) %collective-permute-start.2) | collective-permute-done | bytes 65568 | tf_op jit(solution)/shard_map/ppermute | solution.py:239
  15.6 1.2 %collective-permute-done.3 = bf16[2,128,128]{2,1,0:T(8,128)(2,1)S(1)} collective-permute-done((bf16[2,128,128]{2,1,0:T(8,128)(2,1)}, bf16[2,128,128]{2,1,0:T(8,128)(2,1)S(1)}, u32[]{:S(2)}, u32[]{:S(2)}) %collective-permute-start.3) | collective-permute-done | bytes 65568 | tf_op jit(solution)/shard_map/ppermute | solution.py:239
  16.8 0.9 %pad_maximum_fusion.refs_0_ = bf16[4,2,128,128]{3,2,1,0:T(8,128)(2,1)S(1)} fusion(bf16[1,2,128,128]{3,2,1,0:T(8,128)(2,1)S(1)} %bitcast.8, bf16[1,2,128,128]{3,2,1,0:T(8,128)(2,1)S(1)} %bitcast.7, bf16[1,2,128,128]{3,2,1,0:T(8,128)(2,1)S(1)} %bitcast.6, bf16[1,2,128,128]{3,2,1,0:T(8,128)(2,1)} %bitcast.5), kind=kLoop, calls=%fused_computation.9 | loop fusion | flops 393216 | bytes 524288 | tf_op jit(solution)/shard_map/stack | solution.py:252
  17.7 2.2 %collective-permute-start.4 = (bf16[4,2,128,128]{3,2,1,0:T(8,128)(2,1)S(1)}, bf16[4,2,128,128]{3,2,1,0:T(8,128)(2,1)S(1)}, u32[]{:S(2)}, u32[]{:S(2)}) collective-permute-start(bf16[4,2,128,128]{3,2,1,0:T(8,128)(2,1)S(1)} %pad_maximum_fusion.refs_0_), channel_id=1, source_target_pairs={{0,4},{4,8},{8,12},{12,16},{16,20},{20,24},{24,28},{28,0},{1,5},{5... | collective-permute-start | bytes 786440 | tf_op jit(solution)/shard_map/ppermute | solution.py:253
  19.9 1.1 %collective-permute-start.5 = (bf16[4,2,128,128]{3,2,1,0:T(8,128)(2,1)S(1)}, bf16[4,2,128,128]{3,2,1,0:T(8,128)(2,1)S(1)}, u32[]{:S(2)}, u32[]{:S(2)}) collective-permute-start(bf16[4,2,128,128]{3,2,1,0:T(8,128)(2,1)S(1)} %pad_maximum_fusion.refs_0_), channel_id=1, source_target_pairs={{0,28},{4,0},{8,4},{12,8},{16,12},{20,16},{24,20},{28,24},{1,29},{... | collective-permute-start | bytes 786440 | tf_op jit(solution)/shard_map/ppermute | solution.py:253
  21.0 6.6 %all-to-all-start = ((bf16[16,128,128]{2,1,0:T(8,128)(2,1)}), bf16[16,128,128]{2,1,0:T(8,128)(2,1)S(1)}, u32[]{:S(2)}, u32[]{:S(2)}) async-start(bf16[16,128,128]{2,1,0:T(8,128)(2,1)} %shard_map.55), calls=%async_computation | async-start | bytes 1048576 | tf_op jit(solution)/shard_map/all_to_all | solution.py:250
  27.6 0.0 collective-permute-done.4.refs_1_
  27.6 0.1 collective-permute-start.6
  27.8 0.0 copy-done.1
  27.8 0.1 select_reduce_fusion.2
  27.9 0.0 copy-done
  27.9 0.1 slice_reduce_fusion.1
  28.0 0.1 select_reduce_fusion.1
  28.1 0.4 fusion.3.need_ref
  28.6 0.6 collective-permute-start.7
  29.1 1.5 %shard_map.57.plan_ref = s32[242]{0:T(256)S(1)} custom-call(s32[16]{0:T(128)S(1)} %fusion.3.need_ref, s32[16]{0:T(128)S(1)} %get-tuple-element.42.qblk_ref, s32[24]{0:T(128)S(1)} %get-tuple-element.44.kblk_ref), custom_call_target="tpu_custom_call" | custom-call | flops 1024 | bytes 1024 | tf_op jit(solution)/shard_map/pallas_call | solution.py:298
  30.7 0.0 collective-permute-done.5.refs_2_
  30.7 0.1 collective-permute-start.8
  30.8 0.1 iota_add_fusion
  30.9 0.1 select_reduce_fusion.start_ref
  31.0 0.0 collective-permute-done.6.refs_3_
  31.0 0.0 collective-permute-done.7.refs_4_
  31.0 1.3 %collective-permute-done.8.refs_5_ = bf16[4,2,128,128]{3,2,1,0:T(8,128)(2,1)S(1)} collective-permute-done((bf16[4,2,128,128]{3,2,1,0:T(8,128)(2,1)S(1)}, bf16[4,2,128,128]{3,2,1,0:T(8,128)(2,1)S(1)}, u32[]{:S(2)}, u32[]{:S(2)}) %collective-permute-start.8) | collective-permute-done | bytes 262176 | tf_op jit(solution)/shard_map/ppermute | solution.py:257
  32.3 0.1 shard_map.58.kv_ref
  32.4 4.4 %all-to-all-done.q_ref = bf16[16,128,128]{2,1,0:T(8,128)(2,1)S(1)} async-done(((bf16[16,128,128]{2,1,0:T(8,128)(2,1)}), bf16[16,128,128]{2,1,0:T(8,128)(2,1)S(1)}, u32[]{:S(2)}, u32[]{:S(2)}) %all-to-all-start) | async-done | bytes 524320 | tf_op jit(solution)/shard_map/all_to_all | solution.py:250
  36.8 3.0 %shard_map.59 = bf16[16,144,128]{2,1,0:T(8,128)(2,1)S(1)} custom-call(s32[242]{0:T(256)S(1)} %shard_map.57.plan_ref, s32[16,128]{1,0:T(8,128)S(1)} %select_reduce_fusion.start_ref, bf16[16,128,128]{2,1,0:T(8,128)(2,1)S(1)} %all-to-all-done.q_ref, bf16[24,2,128,128]{3,2,1,0:T(8,128)(2,1)S(1)} %shard_map.58.kv_ref), custom_call_target="tpu_custom_call" | custom-call | tf_op jit(solution)/shard_map/pallas_call | solution.py:306
  39.8 13.8 %all_to_all.10.parts_ref = bf16[16,144,128]{2,1,0:T(8,128)(2,1)S(1)} all-to-all(bf16[16,144,128]{2,1,0:T(8,128)(2,1)S(1)} %shard_map.59), channel_id=1, replica_groups=mesh['x'=4,'c'=2,'z'=8,'y'=4] {'x','y'}, dimensions={0} | all-to-all | bytes 1179648 | tf_op jit(solution)/shard_map/all_to_all | solution.py:319
  53.6 0.2 shard_map.60
  53.8 3.0 %collective-permute-start.9 = (bf16[128,512]{1,0:T(8,128)(2,1)S(1)}, bf16[128,512]{1,0:T(8,128)(2,1)S(1)}, u32[]{:S(2)}, u32[]{:S(2)}) collective-permute-start(bf16[128,512]{1,0:T(8,128)(2,1)S(1)} %shard_map.60), channel_id=1, source_target_pairs={{252,0},{253,1},{254,2},{255,3},{124,4},{125,5},{126,6},{127,7},{1... | collective-permute-start | bytes 393224 | tf_op jit(solution)/shard_map/ppermute | solution.py:328
  56.8 6.6 %collective-permute-done.9 = bf16[128,512]{1,0:T(8,128)(2,1)S(1)} collective-permute-done((bf16[128,512]{1,0:T(8,128)(2,1)S(1)}, bf16[128,512]{1,0:T(8,128)(2,1)S(1)}, u32[]{:S(2)}, u32[]{:S(2)}) %collective-permute-start.9) | collective-permute-done | bytes 131104 | tf_op jit(solution)/shard_map/ppermute | solution.py:328
  63.4 0.7 %copy.7 = bf16[128,512]{1,0:T(8,128)(2,1)} copy(bf16[128,512]{1,0:T(8,128)(2,1)S(1)} %collective-permute-done.9) | data formatting | bytes 262144
  (3 shorter events, 0.0 us)
Async XLA Ops:
  0.0 27.9 %copy-start = (s32[6400,2]{0,1:T(2,128)S(1)}, s32[6400,2]{0,1:T(2,128)}, u32[]{:S(2)}) copy-start(s32[6400,2]{0,1:T(2,128)} %param.8) | copy-start | bytes 153604
  0.0 27.8 %copy-start.1 = (s32[16]{0:T(128)S(1)}, s32[16]{0:T(128)}, u32[]{:S(2)}) copy-start(s32[16]{0:T(128)} %param.9) | copy-start | bytes 196
  0.0 13.7 %collective-permute-start = (bf16[128,512]{1,0:T(8,128)(2,1)}, bf16[128,512]{1,0:T(8,128)(2,1)S(1)}, u32[]{:S(2)}, u32[]{:S(2)}) collective-permute-start(bf16[128,512]{1,0:T(8,128)(2,1)} %param.5), channel_id=1, source_target_pairs={{0,252},{1,253},{2,254},{3,255},{4,124},{5,125},{6,126},{7,127},{8... | collective-permute-start | bytes 393224 | tf_op jit(solution)/shard_map/ppermute | solution.py:238
  7.9 6.7 %collective-permute-start.1 = (bf16[2,128,128]{2,1,0:T(8,128)(2,1)}, bf16[2,128,128]{2,1,0:T(8,128)(2,1)S(1)}, u32[]{:S(2)}, u32[]{:S(2)}) collective-permute-start(bf16[2,128,128]{2,1,0:T(8,128)(2,1)} %get-tuple-element.23), channel_id=1, source_target_pairs={{0,1},{1,2},{2,3},{3,0},{4,5},{5,6},{6,7},{7,4},{8,9},{9,10},{10,1... | collective-permute-start | bytes 196616 | tf_op jit(solution)/shard_map/ppermute | solution.py:239
  9.5 6.2 %collective-permute-start.2 = (bf16[2,128,128]{2,1,0:T(8,128)(2,1)}, bf16[2,128,128]{2,1,0:T(8,128)(2,1)S(1)}, u32[]{:S(2)}, u32[]{:S(2)}) collective-permute-start(bf16[2,128,128]{2,1,0:T(8,128)(2,1)} %get-tuple-element.24), channel_id=1, source_target_pairs={{0,2},{1,3},{2,0},{3,1},{4,6},{5,7},{6,4},{7,5},{8,10},{9,11},{10,... | collective-permute-start | bytes 196616 | tf_op jit(solution)/shard_map/ppermute | solution.py:239
  12.4 4.5 %collective-permute-start.3 = (bf16[2,128,128]{2,1,0:T(8,128)(2,1)}, bf16[2,128,128]{2,1,0:T(8,128)(2,1)S(1)}, u32[]{:S(2)}, u32[]{:S(2)}) collective-permute-start(bf16[2,128,128]{2,1,0:T(8,128)(2,1)} %get-tuple-element.25), channel_id=1, source_target_pairs={{0,3},{1,0},{2,1},{3,2},{4,7},{5,4},{6,5},{7,6},{8,11},{9,8},{10,9... | collective-permute-start | bytes 196616 | tf_op jit(solution)/shard_map/ppermute | solution.py:239
  17.7 9.9 %collective-permute-start.4 = (bf16[4,2,128,128]{3,2,1,0:T(8,128)(2,1)S(1)}, bf16[4,2,128,128]{3,2,1,0:T(8,128)(2,1)S(1)}, u32[]{:S(2)}, u32[]{:S(2)}) collective-permute-start(bf16[4,2,128,128]{3,2,1,0:T(8,128)(2,1)S(1)} %pad_maximum_fusion.refs_0_), channel_id=1, source_target_pairs={{0,4},{4,8},{8,12},{12,16},{16,20},{20,24},{24,28},{28,0},{1,5},{5... | collective-permute-start | bytes 786440 | tf_op jit(solution)/shard_map/ppermute | solution.py:253
  19.9 10.8 %collective-permute-start.5 = (bf16[4,2,128,128]{3,2,1,0:T(8,128)(2,1)S(1)}, bf16[4,2,128,128]{3,2,1,0:T(8,128)(2,1)S(1)}, u32[]{:S(2)}, u32[]{:S(2)}) collective-permute-start(bf16[4,2,128,128]{3,2,1,0:T(8,128)(2,1)S(1)} %pad_maximum_fusion.refs_0_), channel_id=1, source_target_pairs={{0,28},{4,0},{8,4},{12,8},{16,12},{20,16},{24,20},{28,24},{1,29},{... | collective-permute-start | bytes 786440 | tf_op jit(solution)/shard_map/ppermute | solution.py:253
  21.0 15.7 %all-to-all-start = ((bf16[16,128,128]{2,1,0:T(8,128)(2,1)}), bf16[16,128,128]{2,1,0:T(8,128)(2,1)S(1)}, u32[]{:S(2)}, u32[]{:S(2)}) async-start(bf16[16,128,128]{2,1,0:T(8,128)(2,1)} %shard_map.55), calls=%async_computation | async-start | bytes 1048576 | tf_op jit(solution)/shard_map/all_to_all | solution.py:250
  27.6 3.3 %collective-permute-start.6 = (bf16[4,2,128,128]{3,2,1,0:T(8,128)(2,1)S(1)}, bf16[4,2,128,128]{3,2,1,0:T(8,128)(2,1)S(1)}, u32[]{:S(2)}, u32[]{:S(2)}) collective-permute-start(bf16[4,2,128,128]{3,2,1,0:T(8,128)(2,1)S(1)} %pad_maximum_fusion.refs_0_), channel_id=1, source_target_pairs={{0,32},{32,0},{1,33},{33,1},{2,34},{34,2},{3,35},{35,3},{4,36},{36... | collective-permute-start | bytes 786440 | tf_op jit(solution)/shard_map/ppermute | solution.py:257
  28.6 2.4 %collective-permute-start.7 = (bf16[4,2,128,128]{3,2,1,0:T(8,128)(2,1)S(1)}, bf16[4,2,128,128]{3,2,1,0:T(8,128)(2,1)S(1)}, u32[]{:S(2)}, u32[]{:S(2)}) collective-permute-start(bf16[4,2,128,128]{3,2,1,0:T(8,128)(2,1)S(1)} %collective-permute-done.4.refs_1_), channel_id=1, source_target_pairs={{0,32},{32,0},{1,33},{33,1},{2,34},{34,2},{3,35},{35,3},{4,36},{36... | collective-permute-start | bytes 786440 | tf_op jit(solution)/shard_map/ppermute | solution.py:257
  30.7 1.6 %collective-permute-start.8 = (bf16[4,2,128,128]{3,2,1,0:T(8,128)(2,1)S(1)}, bf16[4,2,128,128]{3,2,1,0:T(8,128)(2,1)S(1)}, u32[]{:S(2)}, u32[]{:S(2)}) collective-permute-start(bf16[4,2,128,128]{3,2,1,0:T(8,128)(2,1)S(1)} %collective-permute-done.5.refs_2_), channel_id=1, source_target_pairs={{0,32},{32,0},{1,33},{33,1},{2,34},{34,2},{3,35},{35,3},{4,36},{36... | collective-permute-start | bytes 786440 | tf_op jit(solution)/shard_map/ppermute | solution.py:257
  53.8 9.6 %collective-permute-start.9 = (bf16[128,512]{1,0:T(8,128)(2,1)S(1)}, bf16[128,512]{1,0:T(8,128)(2,1)S(1)}, u32[]{:S(2)}, u32[]{:S(2)}) collective-permute-start(bf16[128,512]{1,0:T(8,128)(2,1)S(1)} %shard_map.60), channel_id=1, source_target_pairs={{252,0},{253,1},{254,2},{255,3},{124,4},{125,5},{126,6},{127,7},{1... | collective-permute-start | bytes 393224 | tf_op jit(solution)/shard_map/ppermute | solution.py:328
where the time goes:
time: 64.7 us; the launch traced here: 64 us
  starting transfers between devices  25.5 us (39%)
  waiting for transfers between devices  14.5 us (22%)
  blocking collectives  13.8 us (21%)
  Pallas kernels  7.54 us (12%)
  other arithmetic  1.25 us (2%)
  local copies, waits for them, and re-layouts  0.78 us (1%)
    all_to_all x1, blocking collectives, on_device(): gathered = lax.all_to_all(parts, ('x', 'y'), 0, 0, tiled=True)  13.8 us
    ppermute x1, waiting for transfers between devices, on_device(): return lax.ppermute(result, ('x', 'c', 'z', 'y'), transpose_pairs(True))  6.63 us
    all_to_all x1, starting transfers between devices, on_device(): mine = lax.all_to_all(spread, ('x', 'y'), 0, 0, tiled=True)  6.61 us
    ppermute x1, starting transfers between devices, on_device(): moved = lax.ppermute(queries, ('x', 'c', 'z', 'y'), transpose_pairs(False))  6.1 us
    ppermute x3, starting transfers between devices, on_device(): lax.ppermute(split[d], 'y', ring(NY, d))  5.83 us
    all_to_all x1, waiting for transfers between devices, on_device(): mine = lax.all_to_all(spread, ('x', 'y'), 0, 0, tiled=True)  4.36 us
    pallas_call x1, Pallas kernels, on_device(): pl.pallas_call(attend_kernel, out_shape=jax.ShapeDtypeStruct((NQ, ROWS, B...  3.01 us
    ppermute x1, starting transfers between devices, on_device(): return lax.ppermute(result, ('x', 'c', 'z', 'y'), transpose_pairs(True))  2.97 us
  transfers between devices with their start and end apart: 11, of which 5 were waited for; matrix products, arithmetic and copies ran while one was open for 1% of the time, Pallas kernels for 7%

commit v1 on v0

--- a/solution.py
+++ b/solution.py
@@ -232,12 +232,15 @@
         out_shape=[piece] * NY,
         in_specs=[SMEM, VMEM, VMEM],
         out_specs=[VMEM] * NY,
-        compiler_params=pltpu.CompilerParams(vmem_limit_bytes=63 << 20),
+        compiler_params=SMALL,
         cost_estimate=LIGHT,
     )(y.reshape(1), keys, values)
     moved = lax.ppermute(queries, ("x", "c", "z", "y"), transpose_pairs(False))
     pieces = [split[0]] + [lax.ppermute(split[d], "y", ring(NY, d)) for d in range(1, NY)]
 
+
+    here = join([p[None] for p in pieces])
+    moved, here = lax.optimization_barrier((moved, here))
     spread = pl.pallas_call(
         pack_queries_kernel,
         out_shape=jax.ShapeDtypeStruct((NQ, DH, BLK), bf16),
@@ -246,10 +249,8 @@
         compiler_params=SMALL,
         cost_estimate=LIGHT,
     )(moved)
-    spread, *pieces = lax.optimization_barrier((spread, *pieces))
     mine = lax.all_to_all(spread, ("x", "y"), 0, 0, tiled=True)
 
-    here = jnp.stack(pieces)
     near = [here, lax.ppermute(here, "z", ring(NZ, 1)), lax.ppermute(here, "z", ring(NZ, -1))]
     near[0], near[1], block_pairs, doc_lengths, x, c, z, y = lax.optimization_barrier(
         (near[0], near[1], block_pairs, doc_lengths, x, c, z, y)

time: 64.7 us -> 64.5 us (level)
  waiting for transfers between devices: 14.5 us -> 18.1 us
  starting transfers between devices: 25.5 us -> 22.8 us
  Pallas kernels: 7.54 us -> 5.09 us
  local copies, waits for them, and re-layouts: 0.78 us -> 2.59 us
  other arithmetic: 1.25 us -> 0.38 us
  blocking collectives: 13.8 us -> 14.6 us
    ppermute x1, starting transfers between devices: 2.97 us -> 0.09 us  [on_device(): return lax.ppermute(result, ('x', 'c', 'z', 'y'), transpose_pairs(True))]
    ppermute x1, waiting for transfers between devices: 6.63 us -> 9.5 us  [on_device(): return lax.ppermute(result, ('x', 'c', 'z', 'y'), transpose_pairs(True))]
    unnamed x5 -> x9, local copies, waits for them, and re-layouts: 0.66 us -> 2.47 us
    pallas_call x1, Pallas kernels: 1.78 us -> 0.12 us  [on_device(): pl.pallas_call(pack_keys_kernel, out_shape=[piece] * NY, in_specs=[SMEM,...]
    another operation x1 -> x0, other arithmetic: 0.87 us -> none  [on_device(): here = jnp.stack(pieces)]
    all_to_all x1, blocking collectives: 13.8 us -> 14.6 us  [on_device(): gathered = lax.all_to_all(parts, ('x', 'y'), 0, 0, tiled=True)]
    pallas_call x1, Pallas kernels: 3.01 us -> 2.24 us  [on_device(): pl.pallas_call(attend_kernel, out_shape=jax.ShapeDtypeStruct((NQ, ROWS, B...]
    ppermute x3, waiting for transfers between devices: 2.21 us -> 2.92 us  [on_device(): lax.ppermute(split[d], 'y', ring(NY, d))]
  transfers between devices with their start and end apart: 11 -> 11, of which waited for: 5 -> 5; matrix products, arithmetic and copies ran while one was open for 1% -> 1% of each run, Pallas kernels for 7% -> 4%
where the time goes in v1:
time: 64.5 us; the launch traced here: 64.1 us
  starting transfers between devices  22.8 us (35%)
  waiting for transfers between devices  18.1 us (28%)
  blocking collectives  14.6 us (23%)
  Pallas kernels  5.09 us (8%)
  local copies, waits for them, and re-layouts  2.59 us (4%)
    all_to_all x1, blocking collectives, on_device(): gathered = lax.all_to_all(parts, ('x', 'y'), 0, 0, tiled=True)  14.6 us
    ppermute x1, waiting for transfers between devices, on_device(): return lax.ppermute(result, ('x', 'c', 'z', 'y'), transpose_pairs(True))  9.5 us
    all_to_all x1, starting transfers between devices, on_device(): mine = lax.all_to_all(spread, ('x', 'y'), 0, 0, tiled=True)  6.61 us
    ppermute x1, starting transfers between devices, on_device(): moved = lax.ppermute(queries, ('x', 'c', 'z', 'y'), transpose_pairs(False))  6.1 us
    ppermute x3, starting transfers between devices, on_device(): lax.ppermute(split[d], 'y', ring(NY, d))  5.9 us
    all_to_all x1, waiting for transfers between devices, on_device(): mine = lax.all_to_all(spread, ('x', 'y'), 0, 0, tiled=True)  4.41 us
    ppermute x3, waiting for transfers between devices, on_device(): lax.ppermute(split[d], 'y', ring(NY, d))  2.92 us
    unnamed x9, local copies, waits for them, and re-layouts  2.47 us
  transfers between devices with their start and end apart: 11, of which 5 were waited for; matrix products, arithmetic and copies ran while one was open for 1% of the time, Pallas kernels for 4%

profile of v1, /device:TPU:6, one launch (start us, length us, event | category | flops | bytes accessed | tf_op | source)
XLA Modules:
  0.0 64.1 jit_solution(12692078370493282864)
XLA Ops:
  0.0 0.0 copy-start.3
  0.0 6.1 %collective-permute-start = (bf16[128,512]{1,0:T(8,128)(2,1)}, bf16[128,512]{1,0:T(8,128)(2,1)S(1)}, u32[]{:S(2)}, u32[]{:S(2)}) collective-permute-start(bf16[128,512]{1,0:T(8,128)(2,1)} %param.5), channel_id=1, source_target_pairs={{0,252},{1,253},{2,254},{3,255},{4,124},{5,125},{6,126},{7,127},{8... | collective-permute-start | bytes 393224 | tf_op jit(solution)/shard_map/ppermute | solution.py:238
  6.1 0.0 copy-start
  6.1 0.9 %copy-done = bf16[128,512]{1,0:T(8,128)(2,1)S(1)} copy-done((bf16[128,512]{1,0:T(8,128)(2,1)S(1)}, bf16[128,512]{1,0:T(8,128)(2,1)}, u32[]{:S(2)}) %copy-start) | copy-done | bytes 131096
  7.0 0.0 copy-start.1
  7.0 0.9 %copy-done.1 = bf16[128,512]{1,0:T(8,128)(2,1)S(1)} copy-done((bf16[128,512]{1,0:T(8,128)(2,1)S(1)}, bf16[128,512]{1,0:T(8,128)(2,1)}, u32[]{:S(2)}) %copy-start.1) | copy-done | bytes 131096
  7.9 0.0 copy-start.2
  7.9 0.1 shard_map.55
  8.0 1.7 %collective-permute-start.1 = (bf16[2,128,128]{2,1,0:T(8,128)(2,1)S(1)}, bf16[2,128,128]{2,1,0:T(8,128)(2,1)S(1)}, u32[]{:S(2)}, u32[]{:S(2)}) collective-permute-start(bf16[2,128,128]{2,1,0:T(8,128)(2,1)S(1)} %get-tuple-element.20), channel_id=1, source_target_pairs={{0,1},{1,2},{2,3},{3,0},{4,5},{5,6},{6,7},{7,4},{8,9},{9,10},{10,1... | collective-permute-start | bytes 196616 | tf_op jit(solution)/shard_map/ppermute | solution.py:239
  9.7 2.9 %collective-permute-start.2 = (bf16[2,128,128]{2,1,0:T(8,128)(2,1)S(1)}, bf16[2,128,128]{2,1,0:T(8,128)(2,1)S(1)}, u32[]{:S(2)}, u32[]{:S(2)}) collective-permute-start(bf16[2,128,128]{2,1,0:T(8,128)(2,1)S(1)} %get-tuple-element.21), channel_id=1, source_target_pairs={{0,2},{1,3},{2,0},{3,1},{4,6},{5,7},{6,4},{7,5},{8,10},{9,11},{10,... | collective-permute-start | bytes 196616 | tf_op jit(solution)/shard_map/ppermute | solution.py:239
  12.6 1.3 %collective-permute-start.3 = (bf16[2,128,128]{2,1,0:T(8,128)(2,1)S(1)}, bf16[2,128,128]{2,1,0:T(8,128)(2,1)S(1)}, u32[]{:S(2)}, u32[]{:S(2)}) collective-permute-start(bf16[2,128,128]{2,1,0:T(8,128)(2,1)S(1)} %get-tuple-element.22), channel_id=1, source_target_pairs={{0,3},{1,0},{2,1},{3,2},{4,7},{5,4},{6,5},{7,6},{8,11},{9,8},{10,9... | collective-permute-start | bytes 196616 | tf_op jit(solution)/shard_map/ppermute | solution.py:239
  13.9 0.0 collective-permute-done.1
  13.9 1.7 %collective-permute-done.2 = bf16[2,128,128]{2,1,0:T(8,128)(2,1)S(1)} collective-permute-done((bf16[2,128,128]{2,1,0:T(8,128)(2,1)S(1)}, bf16[2,128,128]{2,1,0:T(8,128)(2,1)S(1)}, u32[]{:S(2)}, u32[]{:S(2)}) %collective-permute-start.2) | collective-permute-done | bytes 65568 | tf_op jit(solution)/shard_map/ppermute | solution.py:239
  15.6 1.2 %collective-permute-done.3 = bf16[2,128,128]{2,1,0:T(8,128)(2,1)S(1)} collective-permute-done((bf16[2,128,128]{2,1,0:T(8,128)(2,1)S(1)}, bf16[2,128,128]{2,1,0:T(8,128)(2,1)S(1)}, u32[]{:S(2)}, u32[]{:S(2)}) %collective-permute-start.3) | collective-permute-done | bytes 65568 | tf_op jit(solution)/shard_map/ppermute | solution.py:239
  16.9 0.0 collective-permute-done.q_ref
  16.9 2.2 %collective-permute-start.4 = (bf16[4,2,128,128]{3,2,1,0:T(8,128)(2,1)S(1)}, bf16[4,2,128,128]{3,2,1,0:T(8,128)(2,1)S(1)}, u32[]{:S(2)}, u32[]{:S(2)}) collective-permute-start(bf16[4,2,128,128]{3,2,1,0:T(8,128)(2,1)S(1)} %shard_map.56.refs_0_), channel_id=1, source_target_pairs={{0,4},{4,8},{8,12},{12,16},{16,20},{20,24},{24,28},{28,0},{1,5},{5... | collective-permute-start | bytes 786440 | tf_op jit(solution)/shard_map/ppermute | solution.py:254
  19.1 1.1 %collective-permute-start.5 = (bf16[4,2,128,128]{3,2,1,0:T(8,128)(2,1)S(1)}, bf16[4,2,128,128]{3,2,1,0:T(8,128)(2,1)S(1)}, u32[]{:S(2)}, u32[]{:S(2)}) collective-permute-start(bf16[4,2,128,128]{3,2,1,0:T(8,128)(2,1)S(1)} %shard_map.56.refs_0_), channel_id=1, source_target_pairs={{0,28},{4,0},{8,4},{12,8},{16,12},{20,16},{24,20},{28,24},{1,29},{... | collective-permute-start | bytes 786440 | tf_op jit(solution)/shard_map/ppermute | solution.py:254
  20.2 0.9 %shard_map.58 = bf16[16,128,128]{2,1,0:T(8,128)(2,1)} custom-call(bf16[128,512]{1,0:T(8,128)(2,1)S(1)} %collective-permute-done.q_ref), custom_call_target="tpu_custom_call" | custom-call | flops 1024 | bytes 1024 | tf_op jit(solution)/shard_map/pallas_call | solution.py:244
  21.1 6.6 %all-to-all-start = ((bf16[16,128,128]{2,1,0:T(8,128)(2,1)}), bf16[16,128,128]{2,1,0:T(8,128)(2,1)S(1)}, u32[]{:S(2)}, u32[]{:S(2)}) async-start(bf16[16,128,128]{2,1,0:T(8,128)(2,1)} %shard_map.58), calls=%async_computation | async-start | bytes 1048576 | tf_op jit(solution)/shard_map/all_to_all | solution.py:252
  27.7 0.0 collective-permute-done.4.refs_1_
  27.7 0.1 collective-permute-start.6
  27.9 0.0 copy-done.3
  27.9 0.1 select_reduce_fusion.2
  28.0 0.0 copy-done.2
  28.0 0.1 slice_reduce_fusion.1
  28.1 0.1 select_reduce_fusion.1
  28.2 0.4 fusion.3.need_ref
  28.7 0.6 collective-permute-start.7
  29.2 1.5 %shard_map.57.plan_ref = s32[242]{0:T(256)S(1)} custom-call(s32[16]{0:T(128)S(1)} %fusion.3.need_ref, s32[16]{0:T(128)S(1)} %get-tuple-element.36.qblk_ref, s32[24]{0:T(128)S(1)} %get-tuple-element.38.kblk_ref), custom_call_target="tpu_custom_call" | custom-call | flops 1024 | bytes 1024 | tf_op jit(solution)/shard_map/pallas_call | solution.py:299
  30.7 0.0 collective-permute-done.5.refs_2_
  30.7 0.1 collective-permute-start.8
  30.9 0.1 iota_add_fusion
  30.9 0.1 select_reduce_fusion.start_ref
  31.0 0.0 collective-permute-done.6.refs_3_
  31.0 0.0 collective-permute-done.7.refs_4_
  31.0 1.3 %collective-permute-done.8.refs_5_ = bf16[4,2,128,128]{3,2,1,0:T(8,128)(2,1)S(1)} collective-permute-done((bf16[4,2,128,128]{3,2,1,0:T(8,128)(2,1)S(1)}, bf16[4,2,128,128]{3,2,1,0:T(8,128)(2,1)S(1)}, u32[]{:S(2)}, u32[]{:S(2)}) %collective-permute-start.8) | collective-permute-done | bytes 262176 | tf_op jit(solution)/shard_map/ppermute | solution.py:258
  32.4 0.1 shard_map.59.kv_ref
  32.5 4.4 %all-to-all-done.q_ref = bf16[16,128,128]{2,1,0:T(8,128)(2,1)S(1)} async-done(((bf16[16,128,128]{2,1,0:T(8,128)(2,1)}), bf16[16,128,128]{2,1,0:T(8,128)(2,1)S(1)}, u32[]{:S(2)}, u32[]{:S(2)}) %all-to-all-start) | async-done | bytes 524320 | tf_op jit(solution)/shard_map/all_to_all | solution.py:252
  36.9 2.2 %shard_map.60 = bf16[16,144,128]{2,1,0:T(8,128)(2,1)S(1)} custom-call(s32[242]{0:T(256)S(1)} %shard_map.57.plan_ref, s32[16,128]{1,0:T(8,128)S(1)} %select_reduce_fusion.start_ref, bf16[16,128,128]{2,1,0:T(8,128)(2,1)S(1)} %all-to-all-done.q_ref, bf16[24,2,128,128]{3,2,1,0:T(8,128)(2,1)S(1)} %shard_map.59.kv_ref), custom_call_target="tpu_custom_call" | custom-call | tf_op jit(solution)/shard_map/pallas_call | solution.py:307
  39.1 14.6 %all_to_all.10.parts_ref = bf16[16,144,128]{2,1,0:T(8,128)(2,1)S(1)} all-to-all(bf16[16,144,128]{2,1,0:T(8,128)(2,1)S(1)} %shard_map.60), channel_id=1, replica_groups=mesh['x'=4,'c'=2,'z'=8,'y'=4] {'x','y'}, dimensions={0} | all-to-all | bytes 1179648 | tf_op jit(solution)/shard_map/all_to_all | solution.py:320
  53.7 0.2 shard_map.61
  53.9 0.1 collective-permute-start.9
  54.0 9.5 %collective-permute-done.9 = bf16[128,512]{1,0:T(8,128)(2,1)S(1)} collective-permute-done((bf16[128,512]{1,0:T(8,128)(2,1)S(1)}, bf16[128,512]{1,0:T(8,128)(2,1)S(1)}, u32[]{:S(2)}, u32[]{:S(2)}) %collective-permute-start.9) | collective-permute-done | bytes 131104 | tf_op jit(solution)/shard_map/ppermute | solution.py:329
  63.5 0.7 %copy.7 = bf16[128,512]{1,0:T(8,128)(2,1)} copy(bf16[128,512]{1,0:T(8,128)(2,1)S(1)} %collective-permute-done.9) | data formatting | bytes 262144
  (4 shorter events, 0.1 us)
Async XLA Ops:
  0.0 27.9 %copy-start.3 = (s32[16]{0:T(128)S(1)}, s32[16]{0:T(128)}, u32[]{:S(2)}) copy-start(s32[16]{0:T(128)} %param.9) | copy-start | bytes 196
  0.0 16.9 %collective-permute-start = (bf16[128,512]{1,0:T(8,128)(2,1)}, bf16[128,512]{1,0:T(8,128)(2,1)S(1)}, u32[]{:S(2)}, u32[]{:S(2)}) collective-permute-start(bf16[128,512]{1,0:T(8,128)(2,1)} %param.5), channel_id=1, source_target_pairs={{0,252},{1,253},{2,254},{3,255},{4,124},{5,125},{6,126},{7,127},{8... | collective-permute-start | bytes 393224 | tf_op jit(solution)/shard_map/ppermute | solution.py:238
  6.1 0.9 %copy-start = (bf16[128,512]{1,0:T(8,128)(2,1)S(1)}, bf16[128,512]{1,0:T(8,128)(2,1)}, u32[]{:S(2)}) copy-start(bf16[128,512]{1,0:T(8,128)(2,1)} %k_ref.1) | copy-start | bytes 393220
  7.0 0.9 %copy-start.1 = (bf16[128,512]{1,0:T(8,128)(2,1)S(1)}, bf16[128,512]{1,0:T(8,128)(2,1)}, u32[]{:S(2)}) copy-start(bf16[128,512]{1,0:T(8,128)(2,1)} %v_ref.1) | copy-start | bytes 393220
  7.9 20.1 %copy-start.2 = (s32[6400,2]{0,1:T(2,128)S(1)}, s32[6400,2]{0,1:T(2,128)}, u32[]{:S(2)}) copy-start(s32[6400,2]{0,1:T(2,128)} %param.8) | copy-start | bytes 153604
  8.0 5.9 %collective-permute-start.1 = (bf16[2,128,128]{2,1,0:T(8,128)(2,1)S(1)}, bf16[2,128,128]{2,1,0:T(8,128)(2,1)S(1)}, u32[]{:S(2)}, u32[]{:S(2)}) collective-permute-start(bf16[2,128,128]{2,1,0:T(8,128)(2,1)S(1)} %get-tuple-element.20), channel_id=1, source_target_pairs={{0,1},{1,2},{2,3},{3,0},{4,5},{5,6},{6,7},{7,4},{8,9},{9,10},{10,1... | collective-permute-start | bytes 196616 | tf_op jit(solution)/shard_map/ppermute | solution.py:239
  9.7 5.9 %collective-permute-start.2 = (bf16[2,128,128]{2,1,0:T(8,128)(2,1)S(1)}, bf16[2,128,128]{2,1,0:T(8,128)(2,1)S(1)}, u32[]{:S(2)}, u32[]{:S(2)}) collective-permute-start(bf16[2,128,128]{2,1,0:T(8,128)(2,1)S(1)} %get-tuple-element.21), channel_id=1, source_target_pairs={{0,2},{1,3},{2,0},{3,1},{4,6},{5,7},{6,4},{7,5},{8,10},{9,11},{10,... | collective-permute-start | bytes 196616 | tf_op jit(solution)/shard_map/ppermute | solution.py:239
  12.6 4.3 %collective-permute-start.3 = (bf16[2,128,128]{2,1,0:T(8,128)(2,1)S(1)}, bf16[2,128,128]{2,1,0:T(8,128)(2,1)S(1)}, u32[]{:S(2)}, u32[]{:S(2)}) collective-permute-start(bf16[2,128,128]{2,1,0:T(8,128)(2,1)S(1)} %get-tuple-element.22), channel_id=1, source_target_pairs={{0,3},{1,0},{2,1},{3,2},{4,7},{5,4},{6,5},{7,6},{8,11},{9,8},{10,9... | collective-permute-start | bytes 196616 | tf_op jit(solution)/shard_map/ppermute | solution.py:239
  16.9 10.8 %collective-permute-start.4 = (bf16[4,2,128,128]{3,2,1,0:T(8,128)(2,1)S(1)}, bf16[4,2,128,128]{3,2,1,0:T(8,128)(2,1)S(1)}, u32[]{:S(2)}, u32[]{:S(2)}) collective-permute-start(bf16[4,2,128,128]{3,2,1,0:T(8,128)(2,1)S(1)} %shard_map.56.refs_0_), channel_id=1, source_target_pairs={{0,4},{4,8},{8,12},{12,16},{16,20},{20,24},{24,28},{28,0},{1,5},{5... | collective-permute-start | bytes 786440 | tf_op jit(solution)/shard_map/ppermute | solution.py:254
  19.1 11.6 %collective-permute-start.5 = (bf16[4,2,128,128]{3,2,1,0:T(8,128)(2,1)S(1)}, bf16[4,2,128,128]{3,2,1,0:T(8,128)(2,1)S(1)}, u32[]{:S(2)}, u32[]{:S(2)}) collective-permute-start(bf16[4,2,128,128]{3,2,1,0:T(8,128)(2,1)S(1)} %shard_map.56.refs_0_), channel_id=1, source_target_pairs={{0,28},{4,0},{8,4},{12,8},{16,12},{20,16},{24,20},{28,24},{1,29},{... | collective-permute-start | bytes 786440 | tf_op jit(solution)/shard_map/ppermute | solution.py:254
  21.1 15.7 %all-to-all-start = ((bf16[16,128,128]{2,1,0:T(8,128)(2,1)}), bf16[16,128,128]{2,1,0:T(8,128)(2,1)S(1)}, u32[]{:S(2)}, u32[]{:S(2)}) async-start(bf16[16,128,128]{2,1,0:T(8,128)(2,1)} %shard_map.58), calls=%async_computation | async-start | bytes 1048576 | tf_op jit(solution)/shard_map/all_to_all | solution.py:252
  27.7 3.3 %collective-permute-start.6 = (bf16[4,2,128,128]{3,2,1,0:T(8,128)(2,1)S(1)}, bf16[4,2,128,128]{3,2,1,0:T(8,128)(2,1)S(1)}, u32[]{:S(2)}, u32[]{:S(2)}) collective-permute-start(bf16[4,2,128,128]{3,2,1,0:T(8,128)(2,1)S(1)} %shard_map.56.refs_0_), channel_id=1, source_target_pairs={{0,32},{32,0},{1,33},{33,1},{2,34},{34,2},{3,35},{35,3},{4,36},{36... | collective-permute-start | bytes 786440 | tf_op jit(solution)/shard_map/ppermute | solution.py:258
  28.7 2.4 %collective-permute-start.7 = (bf16[4,2,128,128]{3,2,1,0:T(8,128)(2,1)S(1)}, bf16[4,2,128,128]{3,2,1,0:T(8,128)(2,1)S(1)}, u32[]{:S(2)}, u32[]{:S(2)}) collective-permute-start(bf16[4,2,128,128]{3,2,1,0:T(8,128)(2,1)S(1)} %collective-permute-done.4.refs_1_), channel_id=1, source_target_pairs={{0,32},{32,0},{1,33},{33,1},{2,34},{34,2},{3,35},{35,3},{4,36},{36... | collective-permute-start | bytes 786440 | tf_op jit(solution)/shard_map/ppermute | solution.py:258
  30.7 1.6 %collective-permute-start.8 = (bf16[4,2,128,128]{3,2,1,0:T(8,128)(2,1)S(1)}, bf16[4,2,128,128]{3,2,1,0:T(8,128)(2,1)S(1)}, u32[]{:S(2)}, u32[]{:S(2)}) collective-permute-start(bf16[4,2,128,128]{3,2,1,0:T(8,128)(2,1)S(1)} %collective-permute-done.5.refs_2_), channel_id=1, source_target_pairs={{0,32},{32,0},{1,33},{33,1},{2,34},{34,2},{3,35},{35,3},{4,36},{36... | collective-permute-start | bytes 786440 | tf_op jit(solution)/shard_map/ppermute | solution.py:258
  53.9 9.6 %collective-permute-start.9 = (bf16[128,512]{1,0:T(8,128)(2,1)S(1)}, bf16[128,512]{1,0:T(8,128)(2,1)S(1)}, u32[]{:S(2)}, u32[]{:S(2)}) collective-permute-start(bf16[128,512]{1,0:T(8,128)(2,1)S(1)} %shard_map.61), channel_id=1, source_target_pairs={{252,0},{253,1},{254,2},{255,3},{124,4},{125,5},{126,6},{127,7},{1... | collective-permute-start | bytes 393224 | tf_op jit(solution)/shard_map/ppermute | solution.py:329

commit v2 on v1

--- a/solution.py
+++ b/solution.py
@@ -34,14 +34,14 @@
 
 
 PLACE = [
-    [7, 3, 4, 0, 5, 6, 2, 1],
-    [3, 5, 1, 2, 6, 0, 7, 4],
-    [1, 6, 2, 5, 0, 3, 4, 7],
-    [2, 7, 4, 6, 0, 5, 3, 1],
-    [6, 2, 0, 5, 3, 7, 4, 1],
-    [5, 4, 2, 0, 6, 1, 7, 3],
-    [1, 6, 0, 7, 2, 4, 3, 5],
-    [1, 7, 5, 3, 0, 6, 4, 2],
+    [5, 3, 1, 0, 6, 2, 4, 7],
+    [5, 4, 7, 3, 1, 0, 6, 2],
+    [7, 5, 6, 1, 3, 2, 0, 4],
+    [0, 6, 7, 4, 5, 1, 3, 2],
+    [2, 7, 0, 1, 3, 6, 5, 4],
+    [5, 3, 2, 7, 1, 0, 6, 4],
+    [7, 6, 4, 5, 3, 2, 1, 0],
+    [5, 1, 7, 6, 0, 3, 4, 2],
 ]
 LIVES = [
     [
@@ -237,10 +237,9 @@
     )(y.reshape(1), keys, values)
     moved = lax.ppermute(queries, ("x", "c", "z", "y"), transpose_pairs(False))
     pieces = [split[0]] + [lax.ppermute(split[d], "y", ring(NY, d)) for d in range(1, NY)]
-
-
     here = join([p[None] for p in pieces])
     moved, here = lax.optimization_barrier((moved, here))
+
     spread = pl.pallas_call(
         pack_queries_kernel,
         out_shape=jax.ShapeDtypeStruct((NQ, DH, BLK), bf16),
@@ -250,7 +249,6 @@
         cost_estimate=LIGHT,
     )(moved)
     mine = lax.all_to_all(spread, ("x", "y"), 0, 0, tiled=True)
-
     near = [here, lax.ppermute(here, "z", ring(NZ, 1)), lax.ppermute(here, "z", ring(NZ, -1))]
     near[0], near[1], block_pairs, doc_lengths, x, c, z, y = lax.optimization_barrier(
         (near[0], near[1], block_pairs, doc_lengths, x, c, z, y)

time: 64.5 us -> 64.1 us (level)
  the two profiles are of different devices: /device:TPU:6 before, /device:TPU:8 now
where the time goes in v2:
time: 64.1 us; the launch traced here: 63.5 us
  starting transfers between devices  23.1 us (36%)
  waiting for transfers between devices  16.6 us (26%)
  blocking collectives  14.3 us (22%)
  Pallas kernels  5.94 us (9%)
  local copies, waits for them, and re-layouts  2.59 us (4%)
    all_to_all x1, blocking collectives, on_device(): gathered = lax.all_to_all(parts, ('x', 'y'), 0, 0, tiled=True)  14.3 us
    ppermute x1, waiting for transfers between devices, on_device(): return lax.ppermute(result, ('x', 'c', 'z', 'y'), transpose_pairs(True))  8.38 us
    ppermute x1, starting transfers between devices, on_device(): moved = lax.ppermute(queries, ('x', 'c', 'z', 'y'), transpose_pairs(False))  7.76 us
    all_to_all x1, starting transfers between devices, on_device(): mine = lax.all_to_all(spread, ('x', 'y'), 0, 0, tiled=True)  6.18 us
    ppermute x3, starting transfers between devices, on_device(): lax.ppermute(split[d], 'y', ring(NY, d))  5 us
    all_to_all x1, waiting for transfers between devices, on_device(): mine = lax.all_to_all(spread, ('x', 'y'), 0, 0, tiled=True)  4.38 us
    ppermute x1, starting transfers between devices, on_device(): lax.ppermute(here, 'z', ring(NZ, -1))  3.21 us
    pallas_call x1, Pallas kernels, on_device(): pl.pallas_call(attend_kernel, out_shape=jax.ShapeDtypeStruct((NQ, ROWS, B...  3.02 us
  transfers between devices with their start and end apart: 11, of which 4 were waited for; matrix products, arithmetic and copies ran while one was open for 1% of the time, Pallas kernels for 4%

profile of v2, /device:TPU:8, one launch (start us, length us, event | category | flops | bytes accessed | tf_op | source)
XLA Modules:
  0.0 63.5 jit_solution(15714268082353616805)
XLA Ops:
  0.0 0.0 copy-start.3
  0.0 7.8 %collective-permute-start = (bf16[128,512]{1,0:T(8,128)(2,1)}, bf16[128,512]{1,0:T(8,128)(2,1)S(1)}, u32[]{:S(2)}, u32[]{:S(2)}) collective-permute-start(bf16[128,512]{1,0:T(8,128)(2,1)} %param.5), channel_id=1, source_target_pairs={{0,188},{1,189},{2,190},{3,191},{4,124},{5,125},{6,126},{7,127},{8... | collective-permute-start | bytes 393224 | tf_op jit(solution)/shard_map/ppermute | solution.py:238
  7.8 0.0 copy-start
  7.8 0.9 %copy-done = bf16[128,512]{1,0:T(8,128)(2,1)S(1)} copy-done((bf16[128,512]{1,0:T(8,128)(2,1)S(1)}, bf16[128,512]{1,0:T(8,128)(2,1)}, u32[]{:S(2)}) %copy-start) | copy-done | bytes 131096
  8.7 0.0 copy-start.1
  8.7 0.9 %copy-done.1 = bf16[128,512]{1,0:T(8,128)(2,1)S(1)} copy-done((bf16[128,512]{1,0:T(8,128)(2,1)S(1)}, bf16[128,512]{1,0:T(8,128)(2,1)}, u32[]{:S(2)}) %copy-start.1) | copy-done | bytes 131096
  9.6 0.0 copy-start.2
  9.6 0.1 shard_map.55
  9.7 1.7 %collective-permute-start.1 = (bf16[2,128,128]{2,1,0:T(8,128)(2,1)S(1)}, bf16[2,128,128]{2,1,0:T(8,128)(2,1)S(1)}, u32[]{:S(2)}, u32[]{:S(2)}) collective-permute-start(bf16[2,128,128]{2,1,0:T(8,128)(2,1)S(1)} %get-tuple-element.20), channel_id=1, source_target_pairs={{0,1},{1,2},{2,3},{3,0},{4,5},{5,6},{6,7},{7,4},{8,9},{9,10},{10,1... | collective-permute-start | bytes 196616 | tf_op jit(solution)/shard_map/ppermute | solution.py:239
  11.4 0.9 %collective-permute-start.2 = (bf16[2,128,128]{2,1,0:T(8,128)(2,1)S(1)}, bf16[2,128,128]{2,1,0:T(8,128)(2,1)S(1)}, u32[]{:S(2)}, u32[]{:S(2)}) collective-permute-start(bf16[2,128,128]{2,1,0:T(8,128)(2,1)S(1)} %get-tuple-element.21), channel_id=1, source_target_pairs={{0,2},{1,3},{2,0},{3,1},{4,6},{5,7},{6,4},{7,5},{8,10},{9,11},{10,... | collective-permute-start | bytes 196616 | tf_op jit(solution)/shard_map/ppermute | solution.py:239
  12.3 2.4 %collective-permute-start.3 = (bf16[2,128,128]{2,1,0:T(8,128)(2,1)S(1)}, bf16[2,128,128]{2,1,0:T(8,128)(2,1)S(1)}, u32[]{:S(2)}, u32[]{:S(2)}) collective-permute-start(bf16[2,128,128]{2,1,0:T(8,128)(2,1)S(1)} %get-tuple-element.22), channel_id=1, source_target_pairs={{0,3},{1,0},{2,1},{3,2},{4,7},{5,4},{6,5},{7,6},{8,11},{9,8},{10,9... | collective-permute-start | bytes 196616 | tf_op jit(solution)/shard_map/ppermute | solution.py:239
  14.7 0.0 collective-permute-done.1
  14.7 2.5 %collective-permute-done.2 = bf16[2,128,128]{2,1,0:T(8,128)(2,1)S(1)} collective-permute-done((bf16[2,128,128]{2,1,0:T(8,128)(2,1)S(1)}, bf16[2,128,128]{2,1,0:T(8,128)(2,1)S(1)}, u32[]{:S(2)}, u32[]{:S(2)}) %collective-permute-start.2) | collective-permute-done | bytes 65568 | tf_op jit(solution)/shard_map/ppermute | solution.py:239
  17.2 0.0 collective-permute-done.3
  17.3 0.0 collective-permute-done.q_ref
  17.3 0.1 collective-permute-start.4
  17.4 3.2 %collective-permute-start.5 = (bf16[4,2,128,128]{3,2,1,0:T(8,128)(2,1)S(1)}, bf16[4,2,128,128]{3,2,1,0:T(8,128)(2,1)S(1)}, u32[]{:S(2)}, u32[]{:S(2)}) collective-permute-start(bf16[4,2,128,128]{3,2,1,0:T(8,128)(2,1)S(1)} %shard_map.56.refs_0_), channel_id=1, source_target_pairs={{0,28},{4,0},{8,4},{12,8},{16,12},{20,16},{24,20},{28,24},{1,29},{... | collective-permute-start | bytes 786440 | tf_op jit(solution)/shard_map/ppermute | solution.py:252
  20.6 0.9 %shard_map.58 = bf16[16,128,128]{2,1,0:T(8,128)(2,1)} custom-call(bf16[128,512]{1,0:T(8,128)(2,1)S(1)} %collective-permute-done.q_ref), custom_call_target="tpu_custom_call" | custom-call | flops 1024 | bytes 1024 | tf_op jit(solution)/shard_map/pallas_call | solution.py:243
  21.5 6.2 %all-to-all-start = ((bf16[16,128,128]{2,1,0:T(8,128)(2,1)}), bf16[16,128,128]{2,1,0:T(8,128)(2,1)S(1)}, u32[]{:S(2)}, u32[]{:S(2)}) async-start(bf16[16,128,128]{2,1,0:T(8,128)(2,1)} %shard_map.58), calls=%async_computation | async-start | bytes 1048576 | tf_op jit(solution)/shard_map/all_to_all | solution.py:251
  27.7 0.0 collective-permute-done.4.refs_1_
  27.7 0.1 collective-permute-start.6
  27.8 0.0 copy-done.3
  27.9 0.1 select_reduce_fusion.2
  27.9 0.0 copy-done.2
  27.9 0.1 slice_reduce_fusion.1
  28.1 0.1 select_reduce_fusion.1
  28.2 0.4 fusion.3.need_ref
  28.6 0.6 collective-permute-start.7
  29.2 1.6 %shard_map.57.plan_ref = s32[242]{0:T(256)S(1)} custom-call(s32[16]{0:T(128)S(1)} %fusion.3.need_ref, s32[16]{0:T(128)S(1)} %get-tuple-element.36.qblk_ref, s32[24]{0:T(128)S(1)} %get-tuple-element.38.kblk_ref), custom_call_target="tpu_custom_call" | custom-call | flops 1024 | bytes 1024 | tf_op jit(solution)/shard_map/pallas_call | solution.py:297
  30.8 0.0 collective-permute-done.5.refs_2_
  30.8 0.2 collective-permute-start.8
  31.0 0.1 iota_add_fusion
  31.0 0.1 select_reduce_fusion.start_ref
  31.1 0.0 collective-permute-done.6.refs_3_
  31.1 0.0 collective-permute-done.7.refs_4_
  31.2 1.2 %collective-permute-done.8.refs_5_ = bf16[4,2,128,128]{3,2,1,0:T(8,128)(2,1)S(1)} collective-permute-done((bf16[4,2,128,128]{3,2,1,0:T(8,128)(2,1)S(1)}, bf16[4,2,128,128]{3,2,1,0:T(8,128)(2,1)S(1)}, u32[]{:S(2)}, u32[]{:S(2)}) %collective-permute-start.8) | collective-permute-done | bytes 262176 | tf_op jit(solution)/shard_map/ppermute | solution.py:256
  32.4 0.1 shard_map.59.kv_ref
  32.5 4.4 %all-to-all-done.q_ref = bf16[16,128,128]{2,1,0:T(8,128)(2,1)S(1)} async-done(((bf16[16,128,128]{2,1,0:T(8,128)(2,1)}), bf16[16,128,128]{2,1,0:T(8,128)(2,1)S(1)}, u32[]{:S(2)}, u32[]{:S(2)}) %all-to-all-start) | async-done | bytes 524320 | tf_op jit(solution)/shard_map/all_to_all | solution.py:251
  36.9 3.0 %shard_map.60 = bf16[16,144,128]{2,1,0:T(8,128)(2,1)S(1)} custom-call(s32[242]{0:T(256)S(1)} %shard_map.57.plan_ref, s32[16,128]{1,0:T(8,128)S(1)} %select_reduce_fusion.start_ref, bf16[16,128,128]{2,1,0:T(8,128)(2,1)S(1)} %all-to-all-done.q_ref, bf16[24,2,128,128]{3,2,1,0:T(8,128)(2,1)S(1)} %shard_map.59.kv_ref), custom_call_target="tpu_custom_call" | custom-call | tf_op jit(solution)/shard_map/pallas_call | solution.py:305
  39.9 14.3 %all_to_all.10.parts_ref = bf16[16,144,128]{2,1,0:T(8,128)(2,1)S(1)} all-to-all(bf16[16,144,128]{2,1,0:T(8,128)(2,1)S(1)} %shard_map.60), channel_id=1, replica_groups=mesh['x'=4,'c'=2,'z'=8,'y'=4] {'x','y'}, dimensions={0} | all-to-all | bytes 1179648 | tf_op jit(solution)/shard_map/all_to_all | solution.py:318
  54.2 0.2 shard_map.61
  54.4 0.1 collective-permute-start.9
  54.5 8.4 %collective-permute-done.9 = bf16[128,512]{1,0:T(8,128)(2,1)S(1)} collective-permute-done((bf16[128,512]{1,0:T(8,128)(2,1)S(1)}, bf16[128,512]{1,0:T(8,128)(2,1)S(1)}, u32[]{:S(2)}, u32[]{:S(2)}) %collective-permute-start.9) | collective-permute-done | bytes 131104 | tf_op jit(solution)/shard_map/ppermute | solution.py:327
  62.9 0.7 %copy.7 = bf16[128,512]{1,0:T(8,128)(2,1)} copy(bf16[128,512]{1,0:T(8,128)(2,1)S(1)} %collective-permute-done.9) | data formatting | bytes 262144
  (4 shorter events, 0.1 us)
Async XLA Ops:
  0.0 27.8 %copy-start.3 = (s32[16]{0:T(128)S(1)}, s32[16]{0:T(128)}, u32[]{:S(2)}) copy-start(s32[16]{0:T(128)} %param.9) | copy-start | bytes 196
  0.0 17.3 %collective-permute-start = (bf16[128,512]{1,0:T(8,128)(2,1)}, bf16[128,512]{1,0:T(8,128)(2,1)S(1)}, u32[]{:S(2)}, u32[]{:S(2)}) collective-permute-start(bf16[128,512]{1,0:T(8,128)(2,1)} %param.5), channel_id=1, source_target_pairs={{0,188},{1,189},{2,190},{3,191},{4,124},{5,125},{6,126},{7,127},{8... | collective-permute-start | bytes 393224 | tf_op jit(solution)/shard_map/ppermute | solution.py:238
  7.8 0.9 %copy-start = (bf16[128,512]{1,0:T(8,128)(2,1)S(1)}, bf16[128,512]{1,0:T(8,128)(2,1)}, u32[]{:S(2)}) copy-start(bf16[128,512]{1,0:T(8,128)(2,1)} %k_ref.1) | copy-start | bytes 393220
  8.7 0.9 %copy-start.1 = (bf16[128,512]{1,0:T(8,128)(2,1)S(1)}, bf16[128,512]{1,0:T(8,128)(2,1)}, u32[]{:S(2)}) copy-start(bf16[128,512]{1,0:T(8,128)(2,1)} %v_ref.1) | copy-start | bytes 393220
  9.6 18.4 %copy-start.2 = (s32[6400,2]{0,1:T(2,128)S(1)}, s32[6400,2]{0,1:T(2,128)}, u32[]{:S(2)}) copy-start(s32[6400,2]{0,1:T(2,128)} %param.8) | copy-start | bytes 153604
  9.7 5.0 %collective-permute-start.1 = (bf16[2,128,128]{2,1,0:T(8,128)(2,1)S(1)}, bf16[2,128,128]{2,1,0:T(8,128)(2,1)S(1)}, u32[]{:S(2)}, u32[]{:S(2)}) collective-permute-start(bf16[2,128,128]{2,1,0:T(8,128)(2,1)S(1)} %get-tuple-element.20), channel_id=1, source_target_pairs={{0,1},{1,2},{2,3},{3,0},{4,5},{5,6},{6,7},{7,4},{8,9},{9,10},{10,1... | collective-permute-start | bytes 196616 | tf_op jit(solution)/shard_map/ppermute | solution.py:239
  11.4 5.9 %collective-permute-start.2 = (bf16[2,128,128]{2,1,0:T(8,128)(2,1)S(1)}, bf16[2,128,128]{2,1,0:T(8,128)(2,1)S(1)}, u32[]{:S(2)}, u32[]{:S(2)}) collective-permute-start(bf16[2,128,128]{2,1,0:T(8,128)(2,1)S(1)} %get-tuple-element.21), channel_id=1, source_target_pairs={{0,2},{1,3},{2,0},{3,1},{4,6},{5,7},{6,4},{7,5},{8,10},{9,11},{10,... | collective-permute-start | bytes 196616 | tf_op jit(solution)/shard_map/ppermute | solution.py:239
  12.3 5.0 %collective-permute-start.3 = (bf16[2,128,128]{2,1,0:T(8,128)(2,1)S(1)}, bf16[2,128,128]{2,1,0:T(8,128)(2,1)S(1)}, u32[]{:S(2)}, u32[]{:S(2)}) collective-permute-start(bf16[2,128,128]{2,1,0:T(8,128)(2,1)S(1)} %get-tuple-element.22), channel_id=1, source_target_pairs={{0,3},{1,0},{2,1},{3,2},{4,7},{5,4},{6,5},{7,6},{8,11},{9,8},{10,9... | collective-permute-start | bytes 196616 | tf_op jit(solution)/shard_map/ppermute | solution.py:239
  17.3 10.4 %collective-permute-start.4 = (bf16[4,2,128,128]{3,2,1,0:T(8,128)(2,1)S(1)}, bf16[4,2,128,128]{3,2,1,0:T(8,128)(2,1)S(1)}, u32[]{:S(2)}, u32[]{:S(2)}) collective-permute-start(bf16[4,2,128,128]{3,2,1,0:T(8,128)(2,1)S(1)} %shard_map.56.refs_0_), channel_id=1, source_target_pairs={{0,4},{4,8},{8,12},{12,16},{16,20},{20,24},{24,28},{28,0},{1,5},{5... | collective-permute-start | bytes 786440 | tf_op jit(solution)/shard_map/ppermute | solution.py:252
  17.4 13.4 %collective-permute-start.5 = (bf16[4,2,128,128]{3,2,1,0:T(8,128)(2,1)S(1)}, bf16[4,2,128,128]{3,2,1,0:T(8,128)(2,1)S(1)}, u32[]{:S(2)}, u32[]{:S(2)}) collective-permute-start(bf16[4,2,128,128]{3,2,1,0:T(8,128)(2,1)S(1)} %shard_map.56.refs_0_), channel_id=1, source_target_pairs={{0,28},{4,0},{8,4},{12,8},{16,12},{20,16},{24,20},{28,24},{1,29},{... | collective-permute-start | bytes 786440 | tf_op jit(solution)/shard_map/ppermute | solution.py:252
  21.5 15.4 %all-to-all-start = ((bf16[16,128,128]{2,1,0:T(8,128)(2,1)}), bf16[16,128,128]{2,1,0:T(8,128)(2,1)S(1)}, u32[]{:S(2)}, u32[]{:S(2)}) async-start(bf16[16,128,128]{2,1,0:T(8,128)(2,1)} %shard_map.58), calls=%async_computation | async-start | bytes 1048576 | tf_op jit(solution)/shard_map/all_to_all | solution.py:251
  27.7 3.4 %collective-permute-start.6 = (bf16[4,2,128,128]{3,2,1,0:T(8,128)(2,1)S(1)}, bf16[4,2,128,128]{3,2,1,0:T(8,128)(2,1)S(1)}, u32[]{:S(2)}, u32[]{:S(2)}) collective-permute-start(bf16[4,2,128,128]{3,2,1,0:T(8,128)(2,1)S(1)} %shard_map.56.refs_0_), channel_id=1, source_target_pairs={{0,32},{32,0},{1,33},{33,1},{2,34},{34,2},{3,35},{35,3},{4,36},{36... | collective-permute-start | bytes 786440 | tf_op jit(solution)/shard_map/ppermute | solution.py:256
  28.6 2.5 %collective-permute-start.7 = (bf16[4,2,128,128]{3,2,1,0:T(8,128)(2,1)S(1)}, bf16[4,2,128,128]{3,2,1,0:T(8,128)(2,1)S(1)}, u32[]{:S(2)}, u32[]{:S(2)}) collective-permute-start(bf16[4,2,128,128]{3,2,1,0:T(8,128)(2,1)S(1)} %collective-permute-done.4.refs_1_), channel_id=1, source_target_pairs={{0,32},{32,0},{1,33},{33,1},{2,34},{34,2},{3,35},{35,3},{4,36},{36... | collective-permute-start | bytes 786440 | tf_op jit(solution)/shard_map/ppermute | solution.py:256
  30.8 1.6 %collective-permute-start.8 = (bf16[4,2,128,128]{3,2,1,0:T(8,128)(2,1)S(1)}, bf16[4,2,128,128]{3,2,1,0:T(8,128)(2,1)S(1)}, u32[]{:S(2)}, u32[]{:S(2)}) collective-permute-start(bf16[4,2,128,128]{3,2,1,0:T(8,128)(2,1)S(1)} %collective-permute-done.5.refs_2_), channel_id=1, source_target_pairs={{0,32},{32,0},{1,33},{33,1},{2,34},{34,2},{3,35},{35,3},{4,36},{36... | collective-permute-start | bytes 786440 | tf_op jit(solution)/shard_map/ppermute | solution.py:256
  54.4 8.5 %collective-permute-start.9 = (bf16[128,512]{1,0:T(8,128)(2,1)S(1)}, bf16[128,512]{1,0:T(8,128)(2,1)S(1)}, u32[]{:S(2)}, u32[]{:S(2)}) collective-permute-start(bf16[128,512]{1,0:T(8,128)(2,1)S(1)} %shard_map.61), channel_id=1, source_target_pairs={{188,0},{189,1},{190,2},{191,3},{124,4},{125,5},{126,6},{127,7},{6... | collective-permute-start | bytes 393224 | tf_op jit(solution)/shard_map/ppermute | solution.py:327

commit v3 on v2

--- a/solution.py
+++ b/solution.py
@@ -19,7 +19,7 @@
 NK = PLANES * NY * NC
 STAT_ROWS = 16
 ROWS = DH + STAT_ROWS
-UNROLL = 8
+UNROLL = 16
 COUNT_AT = NQ * NK // 2 + UNROLL
 QUERY_AT = COUNT_AT + 1
 KEY_AT = QUERY_AT + NQ
@@ -76,7 +76,16 @@
             out_ref[x * H + h] = part
 
 
-def pack_keys_kernel(y_ref, k_ref, v_ref, *out_refs):
+def pack_keys_kernel(y_ref, k_hbm, v_hbm, *refs):
+    out_refs, (k_ref, v_ref, sems) = refs[:NY], refs[NY:]
+    copies = [
+        pltpu.make_async_copy(v_hbm, v_ref, sems.at[0]),
+        pltpu.make_async_copy(k_hbm, k_ref, sems.at[1]),
+    ]
+    for copy in copies:
+        copy.start()
+    for copy in copies:
+        copy.wait()
     for d, out_ref in enumerate(out_refs):
         at = pl.ds(pl.multiple_of(lax.rem(y_ref[0] + d, H) * DH, DH), DH)
         out_ref[0] = k_ref[:, at]
@@ -219,6 +228,7 @@
 VMEM = pl.BlockSpec(memory_space=pltpu.VMEM)
 SMEM = pl.BlockSpec(memory_space=pltpu.SMEM)
 LIGHT = pl.CostEstimate(flops=1024, bytes_accessed=1024, transcendentals=0)
+HBM = pl.BlockSpec(memory_space=pltpu.HBM)
 SMALL = pltpu.CompilerParams(vmem_limit_bytes=8 << 20)
 
 
@@ -230,11 +240,16 @@
     split = pl.pallas_call(
         pack_keys_kernel,
         out_shape=[piece] * NY,
-        in_specs=[SMEM, VMEM, VMEM],
+        in_specs=[SMEM, HBM, HBM],
         out_specs=[VMEM] * NY,
-        compiler_params=SMALL,
-        cost_estimate=LIGHT,
-    )(y.reshape(1), keys, values)
+        scratch_shapes=[pltpu.VMEM((BLK, H * DH), bf16)] * 2 + [pltpu.SemaphoreType.DMA((2,))],
+        compiler_params=SMALL,
+        cost_estimate=LIGHT,
+    )(
+        y.reshape(1),
+        pltpu.with_memory_space_constraint(keys, pltpu.HBM),
+        pltpu.with_memory_space_constraint(values, pltpu.HBM),
+    )
     moved = lax.ppermute(queries, ("x", "c", "z", "y"), transpose_pairs(False))
     pieces = [split[0]] + [lax.ppermute(split[d], "y", ring(NY, d)) for d in range(1, NY)]
     here = join([p[None] for p in pieces])

time: 64.1 us -> 63.8 us (level); the launches traced: 63.5 us -> 64.1 us
  local copies, waits for them, and re-layouts: 2.59 us -> 0.78 us
  blocking collectives: 14.3 us -> 15.6 us
  waiting for transfers between devices: 16.6 us -> 17.7 us
    unnamed x9 -> x5, local copies, waits for them, and re-layouts: 2.47 us -> 0.66 us
    all_to_all x1, blocking collectives: 14.3 us -> 15.6 us  [on_device(): gathered = lax.all_to_all(parts, ('x', 'y'), 0, 0, tiled=True)]
    pallas_call x1, Pallas kernels: 0.12 us -> 1.11 us  [on_device(): pl.pallas_call(pack_keys_kernel, out_shape=[piece] * NY, in_specs=[SMEM,...]
    pallas_call x1, Pallas kernels: 3.02 us -> 2.06 us  [on_device(): pl.pallas_call(attend_kernel, out_shape=jax.ShapeDtypeStruct((NQ, ROWS, B...]
    all_to_all x1, waiting for transfers between devices: 4.38 us -> 5.29 us  [on_device(): mine = lax.all_to_all(spread, ('x', 'y'), 0, 0, tiled=True)]
  transfers between devices with their start and end apart: 11 -> 11, of which waited for: 4 -> 4; matrix products, arithmetic and copies ran while one was open for 1% -> 1% of each run, Pallas kernels for 4% -> 6%
where the time goes in v3:
time: 63.8 us; the launch traced here: 64.1 us
  starting transfers between devices  23.2 us (36%)
  waiting for transfers between devices  17.7 us (28%)
  blocking collectives  15.6 us (24%)
  Pallas kernels  5.88 us (9%)
  local copies, waits for them, and re-layouts  0.78 us (1%)
    all_to_all x1, blocking collectives, on_device(): gathered = lax.all_to_all(parts, ('x', 'y'), 0, 0, tiled=True)  15.6 us
    ppermute x1, waiting for transfers between devices, on_device(): return lax.ppermute(result, ('x', 'c', 'z', 'y'), transpose_pairs(True))  8.59 us
    ppermute x1, starting transfers between devices, on_device(): moved = lax.ppermute(queries, ('x', 'c', 'z', 'y'), transpose_pairs(False))  7.76 us
    all_to_all x1, starting transfers between devices, on_device(): mine = lax.all_to_all(spread, ('x', 'y'), 0, 0, tiled=True)  6.18 us
    all_to_all x1, waiting for transfers between devices, on_device(): mine = lax.all_to_all(spread, ('x', 'y'), 0, 0, tiled=True)  5.29 us
    ppermute x3, starting transfers between devices, on_device(): lax.ppermute(split[d], 'y', ring(NY, d))  5 us
    ppermute x1, starting transfers between devices, on_device(): lax.ppermute(here, 'z', ring(NZ, -1))  3.21 us
    ppermute x3, waiting for transfers between devices, on_device(): lax.ppermute(split[d], 'y', ring(NY, d))  2.56 us
  transfers between devices with their start and end apart: 11, of which 4 were waited for; matrix products, arithmetic and copies ran while one was open for 1% of the time, Pallas kernels for 6%

profile of v3, /device:TPU:8, one launch (start us, length us, event | category | flops | bytes accessed | tf_op | source)
XLA Modules:
  0.0 64.1 jit_solution(651545257457282026)
XLA Ops:
  0.0 0.0 copy-start
  0.0 0.0 copy-start.1
  0.0 7.8 %collective-permute-start = (bf16[128,512]{1,0:T(8,128)(2,1)}, bf16[128,512]{1,0:T(8,128)(2,1)S(1)}, u32[]{:S(2)}, u32[]{:S(2)}) collective-permute-start(bf16[128,512]{1,0:T(8,128)(2,1)} %param.5), channel_id=1, source_target_pairs={{0,188},{1,189},{2,190},{3,191},{4,124},{5,125},{6,126},{7,127},{8... | collective-permute-start | bytes 393224 | tf_op jit(solution)/shard_map/ppermute | solution.py:253
  7.8 1.1 %shard_map.55 = (bf16[2,128,128]{2,1,0:T(8,128)(2,1)S(1)}, bf16[2,128,128]{2,1,0:T(8,128)(2,1)S(1)}, bf16[2,128,128]{2,1,0:T(8,128)(2,1)S(1)}, bf16[2,128,128]{2,1,0:T(8,128)(2,1)S(1)}) custom-call(s32[1]{0:T(128)} %bitcast.y_ref, bf16[128,512]{1,0:T(8,128)(2,1)} %k_hbm.1, bf16[128,512]{1,0:T(8,128)(2,1)} %v_hbm.1), custom_call_target="tpu_custom_call" | custom-call | flops 1024 | bytes 1024 | tf_op jit(solution)/shard_map/pallas_call | solution.py:240
  8.9 1.7 %collective-permute-start.1 = (bf16[2,128,128]{2,1,0:T(8,128)(2,1)S(1)}, bf16[2,128,128]{2,1,0:T(8,128)(2,1)S(1)}, u32[]{:S(2)}, u32[]{:S(2)}) collective-permute-start(bf16[2,128,128]{2,1,0:T(8,128)(2,1)S(1)} %get-tuple-element.20), channel_id=1, source_target_pairs={{0,1},{1,2},{2,3},{3,0},{4,5},{5,6},{6,7},{7,4},{8,9},{9,10},{10,1... | collective-permute-start | bytes 196616 | tf_op jit(solution)/shard_map/ppermute | solution.py:254
  10.5 0.9 %collective-permute-start.2 = (bf16[2,128,128]{2,1,0:T(8,128)(2,1)S(1)}, bf16[2,128,128]{2,1,0:T(8,128)(2,1)S(1)}, u32[]{:S(2)}, u32[]{:S(2)}) collective-permute-start(bf16[2,128,128]{2,1,0:T(8,128)(2,1)S(1)} %get-tuple-element.21), channel_id=1, source_target_pairs={{0,2},{1,3},{2,0},{3,1},{4,6},{5,7},{6,4},{7,5},{8,10},{9,11},{10,... | collective-permute-start | bytes 196616 | tf_op jit(solution)/shard_map/ppermute | solution.py:254
  11.5 2.4 %collective-permute-start.3 = (bf16[2,128,128]{2,1,0:T(8,128)(2,1)S(1)}, bf16[2,128,128]{2,1,0:T(8,128)(2,1)S(1)}, u32[]{:S(2)}, u32[]{:S(2)}) collective-permute-start(bf16[2,128,128]{2,1,0:T(8,128)(2,1)S(1)} %get-tuple-element.22), channel_id=1, source_target_pairs={{0,3},{1,0},{2,1},{3,2},{4,7},{5,4},{6,5},{7,6},{8,11},{9,8},{10,9... | collective-permute-start | bytes 196616 | tf_op jit(solution)/shard_map/ppermute | solution.py:254
  13.9 0.0 collective-permute-done.1
  13.9 2.5 %collective-permute-done.2 = bf16[2,128,128]{2,1,0:T(8,128)(2,1)S(1)} collective-permute-done((bf16[2,128,128]{2,1,0:T(8,128)(2,1)S(1)}, bf16[2,128,128]{2,1,0:T(8,128)(2,1)S(1)}, u32[]{:S(2)}, u32[]{:S(2)}) %collective-permute-start.2) | collective-permute-done | bytes 65568 | tf_op jit(solution)/shard_map/ppermute | solution.py:254
  16.4 0.0 collective-permute-done.3
  16.5 0.0 collective-permute-done.q_ref
  16.5 0.1 collective-permute-start.4
  16.6 3.2 %collective-permute-start.5 = (bf16[4,2,128,128]{3,2,1,0:T(8,128)(2,1)S(1)}, bf16[4,2,128,128]{3,2,1,0:T(8,128)(2,1)S(1)}, u32[]{:S(2)}, u32[]{:S(2)}) collective-permute-start(bf16[4,2,128,128]{3,2,1,0:T(8,128)(2,1)S(1)} %shard_map.56.refs_0_), channel_id=1, source_target_pairs={{0,28},{4,0},{8,4},{12,8},{16,12},{20,16},{24,20},{28,24},{1,29},{... | collective-permute-start | bytes 786440 | tf_op jit(solution)/shard_map/ppermute | solution.py:267
  19.8 0.9 %shard_map.58 = bf16[16,128,128]{2,1,0:T(8,128)(2,1)} custom-call(bf16[128,512]{1,0:T(8,128)(2,1)S(1)} %collective-permute-done.q_ref), custom_call_target="tpu_custom_call" | custom-call | flops 1024 | bytes 1024 | tf_op jit(solution)/shard_map/pallas_call | solution.py:258
  20.7 6.2 %all-to-all-start = ((bf16[16,128,128]{2,1,0:T(8,128)(2,1)}), bf16[16,128,128]{2,1,0:T(8,128)(2,1)S(1)}, u32[]{:S(2)}, u32[]{:S(2)}) async-start(bf16[16,128,128]{2,1,0:T(8,128)(2,1)} %shard_map.58), calls=%async_computation | async-start | bytes 1048576 | tf_op jit(solution)/shard_map/all_to_all | solution.py:266
  26.9 0.0 collective-permute-done.4.refs_1_
  26.9 0.1 collective-permute-start.6
  27.0 0.0 copy-done.1
  27.0 0.1 select_reduce_fusion.2
  27.1 0.0 copy-done
  27.1 0.1 slice_reduce_fusion.1
  27.3 0.1 select_reduce_fusion.1
  27.4 0.4 fusion.3.need_ref
  27.8 0.6 collective-permute-start.7
  28.4 1.5 %shard_map.57.plan_ref = s32[250]{0:T(256)S(1)} custom-call(s32[16]{0:T(128)S(1)} %fusion.3.need_ref, s32[16]{0:T(128)S(1)} %get-tuple-element.36.qblk_ref, s32[24]{0:T(128)S(1)} %get-tuple-element.38.kblk_ref), custom_call_target="tpu_custom_call" | custom-call | flops 1024 | bytes 1024 | tf_op jit(solution)/shard_map/pallas_call | solution.py:312
  29.9 0.0 collective-permute-done.5.refs_2_
  29.9 0.2 collective-permute-start.8
  30.1 0.1 iota_add_fusion
  30.2 0.1 select_reduce_fusion.start_ref
  30.3 0.0 collective-permute-done.6.refs_3_
  30.3 0.0 collective-permute-done.7.refs_4_
  30.3 1.2 %collective-permute-done.8.refs_5_ = bf16[4,2,128,128]{3,2,1,0:T(8,128)(2,1)S(1)} collective-permute-done((bf16[4,2,128,128]{3,2,1,0:T(8,128)(2,1)S(1)}, bf16[4,2,128,128]{3,2,1,0:T(8,128)(2,1)S(1)}, u32[]{:S(2)}, u32[]{:S(2)}) %collective-permute-start.8) | collective-permute-done | bytes 262176 | tf_op jit(solution)/shard_map/ppermute | solution.py:271
  31.5 0.1 shard_map.59.kv_ref
  31.6 5.3 %all-to-all-done.q_ref = bf16[16,128,128]{2,1,0:T(8,128)(2,1)S(1)} async-done(((bf16[16,128,128]{2,1,0:T(8,128)(2,1)}), bf16[16,128,128]{2,1,0:T(8,128)(2,1)S(1)}, u32[]{:S(2)}, u32[]{:S(2)}) %all-to-all-start) | async-done | bytes 524320 | tf_op jit(solution)/shard_map/all_to_all | solution.py:266
  36.9 2.1 %shard_map.60 = bf16[16,144,128]{2,1,0:T(8,128)(2,1)S(1)} custom-call(s32[250]{0:T(256)S(1)} %shard_map.57.plan_ref, s32[16,128]{1,0:T(8,128)S(1)} %select_reduce_fusion.start_ref, bf16[16,128,128]{2,1,0:T(8,128)(2,1)S(1)} %all-to-all-done.q_ref, bf16[24,2,128,128]{3,2,1,0:T(8,128)(2,1)S(1)} %shard_map.59.kv_ref), custom_call_target="tpu_custom_call" | custom-call | tf_op jit(solution)/shard_map/pallas_call | solution.py:320
  39.0 15.6 %all_to_all.10.parts_ref = bf16[16,144,128]{2,1,0:T(8,128)(2,1)S(1)} all-to-all(bf16[16,144,128]{2,1,0:T(8,128)(2,1)S(1)} %shard_map.60), channel_id=1, replica_groups=mesh['x'=4,'c'=2,'z'=8,'y'=4] {'x','y'}, dimensions={0} | all-to-all | bytes 1179648 | tf_op jit(solution)/shard_map/all_to_all | solution.py:333
  54.5 0.2 shard_map.61
  54.7 0.1 collective-permute-start.9
  54.8 8.6 %collective-permute-done.9 = bf16[128,512]{1,0:T(8,128)(2,1)S(1)} collective-permute-done((bf16[128,512]{1,0:T(8,128)(2,1)S(1)}, bf16[128,512]{1,0:T(8,128)(2,1)S(1)}, u32[]{:S(2)}, u32[]{:S(2)}) %collective-permute-start.9) | collective-permute-done | bytes 131104 | tf_op jit(solution)/shard_map/ppermute | solution.py:342
  63.4 0.7 %copy.7 = bf16[128,512]{1,0:T(8,128)(2,1)} copy(bf16[128,512]{1,0:T(8,128)(2,1)S(1)} %collective-permute-done.9) | data formatting | bytes 262144
  (4 shorter events, 0.1 us)
Async XLA Ops:
  0.0 27.1 %copy-start = (s32[6400,2]{0,1:T(2,128)S(1)}, s32[6400,2]{0,1:T(2,128)}, u32[]{:S(2)}) copy-start(s32[6400,2]{0,1:T(2,128)} %param.8) | copy-start | bytes 153604
  0.0 27.0 %copy-start.1 = (s32[16]{0:T(128)S(1)}, s32[16]{0:T(128)}, u32[]{:S(2)}) copy-start(s32[16]{0:T(128)} %param.9) | copy-start | bytes 196
  0.0 16.5 %collective-permute-start = (bf16[128,512]{1,0:T(8,128)(2,1)}, bf16[128,512]{1,0:T(8,128)(2,1)S(1)}, u32[]{:S(2)}, u32[]{:S(2)}) collective-permute-start(bf16[128,512]{1,0:T(8,128)(2,1)} %param.5), channel_id=1, source_target_pairs={{0,188},{1,189},{2,190},{3,191},{4,124},{5,125},{6,126},{7,127},{8... | collective-permute-start | bytes 393224 | tf_op jit(solution)/shard_map/ppermute | solution.py:253
  8.9 5.0 %collective-permute-start.1 = (bf16[2,128,128]{2,1,0:T(8,128)(2,1)S(1)}, bf16[2,128,128]{2,1,0:T(8,128)(2,1)S(1)}, u32[]{:S(2)}, u32[]{:S(2)}) collective-permute-start(bf16[2,128,128]{2,1,0:T(8,128)(2,1)S(1)} %get-tuple-element.20), channel_id=1, source_target_pairs={{0,1},{1,2},{2,3},{3,0},{4,5},{5,6},{6,7},{7,4},{8,9},{9,10},{10,1... | collective-permute-start | bytes 196616 | tf_op jit(solution)/shard_map/ppermute | solution.py:254
  10.5 5.9 %collective-permute-start.2 = (bf16[2,128,128]{2,1,0:T(8,128)(2,1)S(1)}, bf16[2,128,128]{2,1,0:T(8,128)(2,1)S(1)}, u32[]{:S(2)}, u32[]{:S(2)}) collective-permute-start(bf16[2,128,128]{2,1,0:T(8,128)(2,1)S(1)} %get-tuple-element.21), channel_id=1, source_target_pairs={{0,2},{1,3},{2,0},{3,1},{4,6},{5,7},{6,4},{7,5},{8,10},{9,11},{10,... | collective-permute-start | bytes 196616 | tf_op jit(solution)/shard_map/ppermute | solution.py:254
  11.5 5.0 %collective-permute-start.3 = (bf16[2,128,128]{2,1,0:T(8,128)(2,1)S(1)}, bf16[2,128,128]{2,1,0:T(8,128)(2,1)S(1)}, u32[]{:S(2)}, u32[]{:S(2)}) collective-permute-start(bf16[2,128,128]{2,1,0:T(8,128)(2,1)S(1)} %get-tuple-element.22), channel_id=1, source_target_pairs={{0,3},{1,0},{2,1},{3,2},{4,7},{5,4},{6,5},{7,6},{8,11},{9,8},{10,9... | collective-permute-start | bytes 196616 | tf_op jit(solution)/shard_map/ppermute | solution.py:254
  16.5 10.4 %collective-permute-start.4 = (bf16[4,2,128,128]{3,2,1,0:T(8,128)(2,1)S(1)}, bf16[4,2,128,128]{3,2,1,0:T(8,128)(2,1)S(1)}, u32[]{:S(2)}, u32[]{:S(2)}) collective-permute-start(bf16[4,2,128,128]{3,2,1,0:T(8,128)(2,1)S(1)} %shard_map.56.refs_0_), channel_id=1, source_target_pairs={{0,4},{4,8},{8,12},{12,16},{16,20},{20,24},{24,28},{28,0},{1,5},{5... | collective-permute-start | bytes 786440 | tf_op jit(solution)/shard_map/ppermute | solution.py:267
  16.6 13.3 %collective-permute-start.5 = (bf16[4,2,128,128]{3,2,1,0:T(8,128)(2,1)S(1)}, bf16[4,2,128,128]{3,2,1,0:T(8,128)(2,1)S(1)}, u32[]{:S(2)}, u32[]{:S(2)}) collective-permute-start(bf16[4,2,128,128]{3,2,1,0:T(8,128)(2,1)S(1)} %shard_map.56.refs_0_), channel_id=1, source_target_pairs={{0,28},{4,0},{8,4},{12,8},{16,12},{20,16},{24,20},{28,24},{1,29},{... | collective-permute-start | bytes 786440 | tf_op jit(solution)/shard_map/ppermute | solution.py:267
  20.7 16.2 %all-to-all-start = ((bf16[16,128,128]{2,1,0:T(8,128)(2,1)}), bf16[16,128,128]{2,1,0:T(8,128)(2,1)S(1)}, u32[]{:S(2)}, u32[]{:S(2)}) async-start(bf16[16,128,128]{2,1,0:T(8,128)(2,1)} %shard_map.58), calls=%async_computation | async-start | bytes 1048576 | tf_op jit(solution)/shard_map/all_to_all | solution.py:266
  26.9 3.4 %collective-permute-start.6 = (bf16[4,2,128,128]{3,2,1,0:T(8,128)(2,1)S(1)}, bf16[4,2,128,128]{3,2,1,0:T(8,128)(2,1)S(1)}, u32[]{:S(2)}, u32[]{:S(2)}) collective-permute-start(bf16[4,2,128,128]{3,2,1,0:T(8,128)(2,1)S(1)} %shard_map.56.refs_0_), channel_id=1, source_target_pairs={{0,32},{32,0},{1,33},{33,1},{2,34},{34,2},{3,35},{35,3},{4,36},{36... | collective-permute-start | bytes 786440 | tf_op jit(solution)/shard_map/ppermute | solution.py:271
  27.8 2.5 %collective-permute-start.7 = (bf16[4,2,128,128]{3,2,1,0:T(8,128)(2,1)S(1)}, bf16[4,2,128,128]{3,2,1,0:T(8,128)(2,1)S(1)}, u32[]{:S(2)}, u32[]{:S(2)}) collective-permute-start(bf16[4,2,128,128]{3,2,1,0:T(8,128)(2,1)S(1)} %collective-permute-done.4.refs_1_), channel_id=1, source_target_pairs={{0,32},{32,0},{1,33},{33,1},{2,34},{34,2},{3,35},{35,3},{4,36},{36... | collective-permute-start | bytes 786440 | tf_op jit(solution)/shard_map/ppermute | solution.py:271
  29.9 1.6 %collective-permute-start.8 = (bf16[4,2,128,128]{3,2,1,0:T(8,128)(2,1)S(1)}, bf16[4,2,128,128]{3,2,1,0:T(8,128)(2,1)S(1)}, u32[]{:S(2)}, u32[]{:S(2)}) collective-permute-start(bf16[4,2,128,128]{3,2,1,0:T(8,128)(2,1)S(1)} %collective-permute-done.5.refs_2_), channel_id=1, source_target_pairs={{0,32},{32,0},{1,33},{33,1},{2,34},{34,2},{3,35},{35,3},{4,36},{36... | collective-permute-start | bytes 786440 | tf_op jit(solution)/shard_map/ppermute | solution.py:271
  54.7 8.7 %collective-permute-start.9 = (bf16[128,512]{1,0:T(8,128)(2,1)S(1)}, bf16[128,512]{1,0:T(8,128)(2,1)S(1)}, u32[]{:S(2)}, u32[]{:S(2)}) collective-permute-start(bf16[128,512]{1,0:T(8,128)(2,1)S(1)} %shard_map.61), channel_id=1, source_target_pairs={{188,0},{189,1},{190,2},{191,3},{124,4},{125,5},{126,6},{127,7},{6... | collective-permute-start | bytes 393224 | tf_op jit(solution)/shard_map/ppermute | solution.py:342

commit v4 on v3

--- a/solution.py
+++ b/solution.py
@@ -19,7 +19,7 @@
 NK = PLANES * NY * NC
 STAT_ROWS = 16
 ROWS = DH + STAT_ROWS
-UNROLL = 16
+UNROLL = 8
 COUNT_AT = NQ * NK // 2 + UNROLL
 QUERY_AT = COUNT_AT + 1
 KEY_AT = QUERY_AT + NQ
@@ -33,19 +33,20 @@
     return ((x * NC + c) * NZ + z) * NY + y
 
 
+WORK = [(p - 2) % NZ if p % 2 == 0 else p for p in range(NZ)]
 PLACE = [
-    [5, 3, 1, 0, 6, 2, 4, 7],
-    [5, 4, 7, 3, 1, 0, 6, 2],
-    [7, 5, 6, 1, 3, 2, 0, 4],
-    [0, 6, 7, 4, 5, 1, 3, 2],
-    [2, 7, 0, 1, 3, 6, 5, 4],
-    [5, 3, 2, 7, 1, 0, 6, 4],
-    [7, 6, 4, 5, 3, 2, 1, 0],
-    [5, 1, 7, 6, 0, 3, 4, 2],
+    [7, 2, 0, 1, 6, 4, 3, 5],
+    [4, 5, 6, 2, 3, 1, 0, 7],
+    [1, 7, 0, 4, 2, 3, 5, 6],
+    [2, 0, 7, 4, 6, 5, 1, 3],
+    [7, 1, 3, 0, 2, 6, 4, 5],
+    [4, 5, 3, 2, 0, 6, 1, 7],
+    [6, 7, 1, 5, 3, 2, 4, 0],
+    [3, 0, 1, 7, 6, 4, 2, 5],
 ]
 LIVES = [
     [
-        sum(PLACE[(z + 1) % NZ].index(2 * x + c) << (3 * z) for z in range(NZ))
+        sum(PLACE[WORK.index(z)].index(2 * x + c) << (3 * z) for z in range(NZ))
         for c in range(NC)
     ]
     for x in range(NX)
@@ -60,7 +61,7 @@
                 for y in range(NY):
                     p = 2 * x + c
                     home = device(x, c, z, y)
-                    work = device(PLACE[p][z] // 2, PLACE[p][z] % 2, (p - 1) % NZ, y)
+                    work = device(PLACE[p][z] // 2, PLACE[p][z] % 2, WORK[p], y)
                     pairs.append((work, home) if back else (home, work))
     return pairs
 
@@ -264,7 +265,11 @@
         cost_estimate=LIGHT,
     )(moved)
     mine = lax.all_to_all(spread, ("x", "y"), 0, 0, tiled=True)
-    near = [here, lax.ppermute(here, "z", ring(NZ, 1)), lax.ppermute(here, "z", ring(NZ, -1))]
+    near = [
+        here,
+        lax.ppermute(here, "z", [(i, i ^ 1) for i in range(NZ)]),
+        lax.ppermute(here, "z", [(i, (i + (2 if i % 2 else -2)) % NZ) for i in range(NZ)]),
+    ]
     near[0], near[1], block_pairs, doc_lengths, x, c, z, y = lax.optimization_barrier(
         (near[0], near[1], block_pairs, doc_lengths, x, c, z, y)
     )
@@ -278,10 +283,10 @@
     lives = functools.reduce(
         lambda rest, n: jnp.where(slot // NY == n, digits[n], rest), range(NX), slot
     )
-    query_block = PLANE * lax.rem(z + 1, NZ) + NY * lives + slot % NY
+    query_block = PLANE * jnp.where(z % 2 == 0, lax.rem(z + 2, NZ), z) + NY * lives + slot % NY
     slot = jnp.arange(NK, dtype=jnp.int32)
     group = (slot // NY) % PLANES
-    plane = lax.rem(z + jnp.where(group == 0, 0, jnp.where(group == 1, NZ - 1, 1)), NZ)
+    plane = lax.rem(z + jnp.where(z % 2 == 0, group, (NZ - group) % NZ), NZ)
     row = lax.rem(y + NY - slot % NY, NY)
     core = jnp.where(slot < PLANES * NY, c, 1 - c)
     key_block = PLANE * plane + 8 * row + 2 * x + core

time: 63.8 us -> 65.1 us (1.020); the launches traced: 64.1 us -> 64.4 us
  waiting for transfers between devices: 17.7 us -> 16.6 us
  Pallas kernels: 5.88 us -> 6.93 us
    all_to_all x1, waiting for transfers between devices: 5.29 us -> 4.1 us  [on_device(): mine = lax.all_to_all(spread, ('x', 'y'), 0, 0, tiled=True)]
    pallas_call x1, Pallas kernels: 2.06 us -> 3.01 us  [on_device(): pl.pallas_call(attend_kernel, out_shape=jax.ShapeDtypeStruct((NQ, ROWS, B...]
    ppermute x2, starting transfers between devices: 3.29 us -> 2.4 us  [the longest x1 1.55 us: on_device(): lax.ppermute(here, 'z', [(i, (i + (2 if i % 2 else -2)) % NZ) for i in ra...]
    all_to_all x1, blocking collectives: 15.6 us -> 16.2 us  [on_device(): gathered = lax.all_to_all(parts, ('x', 'y'), 0, 0, tiled=True)]
where the time goes in v4:
time: 65.1 us; the launch traced here: 64.4 us
  starting transfers between devices  22.9 us (35%)
  waiting for transfers between devices  16.6 us (25%)
  blocking collectives  16.2 us (25%)
  Pallas kernels  6.93 us (11%)
  local copies, waits for them, and re-layouts  0.78 us (1%)
    all_to_all x1, blocking collectives, on_device(): gathered = lax.all_to_all(parts, ('x', 'y'), 0, 0, tiled=True)  16.2 us
    ppermute x1, waiting for transfers between devices, on_device(): return lax.ppermute(result, ('x', 'c', 'z', 'y'), transpose_pairs(True))  8.61 us
    ppermute x1, starting transfers between devices, on_device(): moved = lax.ppermute(queries, ('x', 'c', 'z', 'y'), transpose_pairs(False))  7.93 us
    all_to_all x1, starting transfers between devices, on_device(): mine = lax.all_to_all(spread, ('x', 'y'), 0, 0, tiled=True)  6.63 us
    ppermute x3, starting transfers between devices, on_device(): lax.ppermute(split[d], 'y', ring(NY, d))  5 us
    all_to_all x1, waiting for transfers between devices, on_device(): mine = lax.all_to_all(spread, ('x', 'y'), 0, 0, tiled=True)  4.1 us
    pallas_call x1, Pallas kernels, on_device(): pl.pallas_call(attend_kernel, out_shape=jax.ShapeDtypeStruct((NQ, ROWS, B...  3.01 us
    ppermute x3, waiting for transfers between devices, on_device(): lax.ppermute(split[d], 'y', ring(NY, d))  2.56 us
  transfers between devices with their start and end apart: 11, of which 4 were waited for; matrix products, arithmetic and copies ran while one was open for 1% of the time, Pallas kernels for 6%

profile of v4, /device:TPU:8, one launch (start us, length us, event | category | flops | bytes accessed | tf_op | source)
XLA Modules:
  0.0 64.4 jit_solution(14773832539266411014)
XLA Ops:
  0.0 0.0 copy-start
  0.0 0.0 copy-start.1
  0.0 7.9 %collective-permute-start = (bf16[128,512]{1,0:T(8,128)(2,1)}, bf16[128,512]{1,0:T(8,128)(2,1)S(1)}, u32[]{:S(2)}, u32[]{:S(2)}) collective-permute-start(bf16[128,512]{1,0:T(8,128)(2,1)} %param.5), channel_id=1, source_target_pairs={{0,248},{1,249},{2,250},{3,251},{4,88},{5,89},{6,90},{7,91},{8,24}... | collective-permute-start | bytes 393224 | tf_op jit(solution)/shard_map/ppermute | solution.py:254
  7.9 1.1 %shard_map.55 = (bf16[2,128,128]{2,1,0:T(8,128)(2,1)S(1)}, bf16[2,128,128]{2,1,0:T(8,128)(2,1)S(1)}, bf16[2,128,128]{2,1,0:T(8,128)(2,1)S(1)}, bf16[2,128,128]{2,1,0:T(8,128)(2,1)S(1)}) custom-call(s32[1]{0:T(128)} %bitcast.y_ref, bf16[128,512]{1,0:T(8,128)(2,1)} %k_hbm.1, bf16[128,512]{1,0:T(8,128)(2,1)} %v_hbm.1), custom_call_target="tpu_custom_call" | custom-call | flops 1024 | bytes 1024 | tf_op jit(solution)/shard_map/pallas_call | solution.py:241
  9.1 1.7 %collective-permute-start.1 = (bf16[2,128,128]{2,1,0:T(8,128)(2,1)S(1)}, bf16[2,128,128]{2,1,0:T(8,128)(2,1)S(1)}, u32[]{:S(2)}, u32[]{:S(2)}) collective-permute-start(bf16[2,128,128]{2,1,0:T(8,128)(2,1)S(1)} %get-tuple-element.20), channel_id=1, source_target_pairs={{0,1},{1,2},{2,3},{3,0},{4,5},{5,6},{6,7},{7,4},{8,9},{9,10},{10,1... | collective-permute-start | bytes 196616 | tf_op jit(solution)/shard_map/ppermute | solution.py:255
  10.7 0.9 %collective-permute-start.2 = (bf16[2,128,128]{2,1,0:T(8,128)(2,1)S(1)}, bf16[2,128,128]{2,1,0:T(8,128)(2,1)S(1)}, u32[]{:S(2)}, u32[]{:S(2)}) collective-permute-start(bf16[2,128,128]{2,1,0:T(8,128)(2,1)S(1)} %get-tuple-element.21), channel_id=1, source_target_pairs={{0,2},{1,3},{2,0},{3,1},{4,6},{5,7},{6,4},{7,5},{8,10},{9,11},{10,... | collective-permute-start | bytes 196616 | tf_op jit(solution)/shard_map/ppermute | solution.py:255
  11.7 2.4 %collective-permute-start.3 = (bf16[2,128,128]{2,1,0:T(8,128)(2,1)S(1)}, bf16[2,128,128]{2,1,0:T(8,128)(2,1)S(1)}, u32[]{:S(2)}, u32[]{:S(2)}) collective-permute-start(bf16[2,128,128]{2,1,0:T(8,128)(2,1)S(1)} %get-tuple-element.22), channel_id=1, source_target_pairs={{0,3},{1,0},{2,1},{3,2},{4,7},{5,4},{6,5},{7,6},{8,11},{9,8},{10,9... | collective-permute-start | bytes 196616 | tf_op jit(solution)/shard_map/ppermute | solution.py:255
  14.1 0.0 collective-permute-done.1
  14.1 2.5 %collective-permute-done.2 = bf16[2,128,128]{2,1,0:T(8,128)(2,1)S(1)} collective-permute-done((bf16[2,128,128]{2,1,0:T(8,128)(2,1)S(1)}, bf16[2,128,128]{2,1,0:T(8,128)(2,1)S(1)}, u32[]{:S(2)}, u32[]{:S(2)}) %collective-permute-start.2) | collective-permute-done | bytes 65568 | tf_op jit(solution)/shard_map/ppermute | solution.py:255
  16.6 0.0 collective-permute-done.3
  16.6 0.0 collective-permute-done.q_ref
  16.7 0.8 %collective-permute-start.4 = (bf16[4,2,128,128]{3,2,1,0:T(8,128)(2,1)S(1)}, bf16[4,2,128,128]{3,2,1,0:T(8,128)(2,1)S(1)}, u32[]{:S(2)}, u32[]{:S(2)}) collective-permute-start(bf16[4,2,128,128]{3,2,1,0:T(8,128)(2,1)S(1)} %shard_map.56.refs_0_), channel_id=1, source_target_pairs={{0,4},{4,0},{8,12},{12,8},{16,20},{20,16},{24,28},{28,24},{1,5},{5... | collective-permute-start | bytes 786440 | tf_op jit(solution)/shard_map/ppermute | solution.py:270
  17.5 1.6 %collective-permute-start.5 = (bf16[4,2,128,128]{3,2,1,0:T(8,128)(2,1)S(1)}, bf16[4,2,128,128]{3,2,1,0:T(8,128)(2,1)S(1)}, u32[]{:S(2)}, u32[]{:S(2)}) collective-permute-start(bf16[4,2,128,128]{3,2,1,0:T(8,128)(2,1)S(1)} %shard_map.56.refs_0_), channel_id=1, source_target_pairs={{0,24},{4,12},{8,0},{12,20},{16,8},{20,28},{24,16},{28,4},{1,25},{... | collective-permute-start | bytes 786440 | tf_op jit(solution)/shard_map/ppermute | solution.py:271
  19.1 0.9 %shard_map.58 = bf16[16,128,128]{2,1,0:T(8,128)(2,1)} custom-call(bf16[128,512]{1,0:T(8,128)(2,1)S(1)} %collective-permute-done.q_ref), custom_call_target="tpu_custom_call" | custom-call | flops 1024 | bytes 1024 | tf_op jit(solution)/shard_map/pallas_call | solution.py:259
  20.0 6.6 %all-to-all-start = ((bf16[16,128,128]{2,1,0:T(8,128)(2,1)}), bf16[16,128,128]{2,1,0:T(8,128)(2,1)S(1)}, u32[]{:S(2)}, u32[]{:S(2)}) async-start(bf16[16,128,128]{2,1,0:T(8,128)(2,1)} %shard_map.58), calls=%async_computation | async-start | bytes 1048576 | tf_op jit(solution)/shard_map/all_to_all | solution.py:267
  26.6 0.0 collective-permute-done.4.refs_1_
  26.6 0.1 collective-permute-start.6
  26.7 0.0 copy-done.1
  26.7 0.1 select_reduce_fusion.2
  26.8 0.0 copy-done
  26.8 0.1 slice_reduce_fusion.1
  27.0 0.1 select_reduce_fusion.1
  27.1 0.4 fusion.3.need_ref
  27.6 0.6 collective-permute-start.7
  28.1 1.6 %shard_map.57.plan_ref = s32[242]{0:T(256)S(1)} custom-call(s32[16]{0:T(128)S(1)} %fusion.3.need_ref, s32[16]{0:T(128)S(1)} %get-tuple-element.36.qblk_ref, s32[24]{0:T(128)S(1)} %get-tuple-element.38.kblk_ref), custom_call_target="tpu_custom_call" | custom-call | flops 1024 | bytes 1024 | tf_op jit(solution)/shard_map/pallas_call | solution.py:317
  29.7 0.0 collective-permute-done.5.refs_2_
  29.7 0.1 collective-permute-start.8
  29.8 0.1 iota_add_fusion
  29.9 0.1 select_reduce_fusion.start_ref
  30.0 0.0 collective-permute-done.6.refs_3_
  30.0 0.0 collective-permute-done.7.refs_4_
  30.0 1.3 %collective-permute-done.8.refs_5_ = bf16[4,2,128,128]{3,2,1,0:T(8,128)(2,1)S(1)} collective-permute-done((bf16[4,2,128,128]{3,2,1,0:T(8,128)(2,1)S(1)}, bf16[4,2,128,128]{3,2,1,0:T(8,128)(2,1)S(1)}, u32[]{:S(2)}, u32[]{:S(2)}) %collective-permute-start.8) | collective-permute-done | bytes 262176 | tf_op jit(solution)/shard_map/ppermute | solution.py:276
  31.3 0.1 shard_map.59.kv_ref
  31.4 4.1 %all-to-all-done.q_ref = bf16[16,128,128]{2,1,0:T(8,128)(2,1)S(1)} async-done(((bf16[16,128,128]{2,1,0:T(8,128)(2,1)}), bf16[16,128,128]{2,1,0:T(8,128)(2,1)S(1)}, u32[]{:S(2)}, u32[]{:S(2)}) %all-to-all-start) | async-done | bytes 524320 | tf_op jit(solution)/shard_map/all_to_all | solution.py:267
  35.5 3.0 %shard_map.60 = bf16[16,144,128]{2,1,0:T(8,128)(2,1)S(1)} custom-call(s32[242]{0:T(256)S(1)} %shard_map.57.plan_ref, s32[16,128]{1,0:T(8,128)S(1)} %select_reduce_fusion.start_ref, bf16[16,128,128]{2,1,0:T(8,128)(2,1)S(1)} %all-to-all-done.q_ref, bf16[24,2,128,128]{3,2,1,0:T(8,128)(2,1)S(1)} %shard_map.59.kv_ref), custom_call_target="tpu_custom_call" | custom-call | tf_op jit(solution)/shard_map/pallas_call | solution.py:325
  38.6 16.2 %all_to_all.10.parts_ref = bf16[16,144,128]{2,1,0:T(8,128)(2,1)S(1)} all-to-all(bf16[16,144,128]{2,1,0:T(8,128)(2,1)S(1)} %shard_map.60), channel_id=1, replica_groups=mesh['x'=4,'c'=2,'z'=8,'y'=4] {'x','y'}, dimensions={0} | all-to-all | bytes 1179648 | tf_op jit(solution)/shard_map/all_to_all | solution.py:338
  54.8 0.2 shard_map.61
  55.0 0.2 collective-permute-start.9
  55.2 8.6 %collective-permute-done.9 = bf16[128,512]{1,0:T(8,128)(2,1)S(1)} collective-permute-done((bf16[128,512]{1,0:T(8,128)(2,1)S(1)}, bf16[128,512]{1,0:T(8,128)(2,1)S(1)}, u32[]{:S(2)}, u32[]{:S(2)}) %collective-permute-start.9) | collective-permute-done | bytes 131104 | tf_op jit(solution)/shard_map/ppermute | solution.py:347
  63.8 0.7 %copy.7 = bf16[128,512]{1,0:T(8,128)(2,1)} copy(bf16[128,512]{1,0:T(8,128)(2,1)S(1)} %collective-permute-done.9) | data formatting | bytes 262144
  (4 shorter events, 0.1 us)
Async XLA Ops:
  0.0 26.8 %copy-start = (s32[6400,2]{0,1:T(2,128)S(1)}, s32[6400,2]{0,1:T(2,128)}, u32[]{:S(2)}) copy-start(s32[6400,2]{0,1:T(2,128)} %param.8) | copy-start | bytes 153604
  0.0 26.7 %copy-start.1 = (s32[16]{0:T(128)S(1)}, s32[16]{0:T(128)}, u32[]{:S(2)}) copy-start(s32[16]{0:T(128)} %param.9) | copy-start | bytes 196
  0.0 16.6 %collective-permute-start = (bf16[128,512]{1,0:T(8,128)(2,1)}, bf16[128,512]{1,0:T(8,128)(2,1)S(1)}, u32[]{:S(2)}, u32[]{:S(2)}) collective-permute-start(bf16[128,512]{1,0:T(8,128)(2,1)} %param.5), channel_id=1, source_target_pairs={{0,248},{1,249},{2,250},{3,251},{4,88},{5,89},{6,90},{7,91},{8,24}... | collective-permute-start | bytes 393224 | tf_op jit(solution)/shard_map/ppermute | solution.py:254
  9.1 5.0 %collective-permute-start.1 = (bf16[2,128,128]{2,1,0:T(8,128)(2,1)S(1)}, bf16[2,128,128]{2,1,0:T(8,128)(2,1)S(1)}, u32[]{:S(2)}, u32[]{:S(2)}) collective-permute-start(bf16[2,128,128]{2,1,0:T(8,128)(2,1)S(1)} %get-tuple-element.20), channel_id=1, source_target_pairs={{0,1},{1,2},{2,3},{3,0},{4,5},{5,6},{6,7},{7,4},{8,9},{9,10},{10,1... | collective-permute-start | bytes 196616 | tf_op jit(solution)/shard_map/ppermute | solution.py:255
  10.7 5.9 %collective-permute-start.2 = (bf16[2,128,128]{2,1,0:T(8,128)(2,1)S(1)}, bf16[2,128,128]{2,1,0:T(8,128)(2,1)S(1)}, u32[]{:S(2)}, u32[]{:S(2)}) collective-permute-start(bf16[2,128,128]{2,1,0:T(8,128)(2,1)S(1)} %get-tuple-element.21), channel_id=1, source_target_pairs={{0,2},{1,3},{2,0},{3,1},{4,6},{5,7},{6,4},{7,5},{8,10},{9,11},{10,... | collective-permute-start | bytes 196616 | tf_op jit(solution)/shard_map/ppermute | solution.py:255
  11.7 5.0 %collective-permute-start.3 = (bf16[2,128,128]{2,1,0:T(8,128)(2,1)S(1)}, bf16[2,128,128]{2,1,0:T(8,128)(2,1)S(1)}, u32[]{:S(2)}, u32[]{:S(2)}) collective-permute-start(bf16[2,128,128]{2,1,0:T(8,128)(2,1)S(1)} %get-tuple-element.22), channel_id=1, source_target_pairs={{0,3},{1,0},{2,1},{3,2},{4,7},{5,4},{6,5},{7,6},{8,11},{9,8},{10,9... | collective-permute-start | bytes 196616 | tf_op jit(solution)/shard_map/ppermute | solution.py:255
  16.7 9.9 %collective-permute-start.4 = (bf16[4,2,128,128]{3,2,1,0:T(8,128)(2,1)S(1)}, bf16[4,2,128,128]{3,2,1,0:T(8,128)(2,1)S(1)}, u32[]{:S(2)}, u32[]{:S(2)}) collective-permute-start(bf16[4,2,128,128]{3,2,1,0:T(8,128)(2,1)S(1)} %shard_map.56.refs_0_), channel_id=1, source_target_pairs={{0,4},{4,0},{8,12},{12,8},{16,20},{20,16},{24,28},{28,24},{1,5},{5... | collective-permute-start | bytes 786440 | tf_op jit(solution)/shard_map/ppermute | solution.py:270
  17.5 12.2 %collective-permute-start.5 = (bf16[4,2,128,128]{3,2,1,0:T(8,128)(2,1)S(1)}, bf16[4,2,128,128]{3,2,1,0:T(8,128)(2,1)S(1)}, u32[]{:S(2)}, u32[]{:S(2)}) collective-permute-start(bf16[4,2,128,128]{3,2,1,0:T(8,128)(2,1)S(1)} %shard_map.56.refs_0_), channel_id=1, source_target_pairs={{0,24},{4,12},{8,0},{12,20},{16,8},{20,28},{24,16},{28,4},{1,25},{... | collective-permute-start | bytes 786440 | tf_op jit(solution)/shard_map/ppermute | solution.py:271
  20.0 15.6 %all-to-all-start = ((bf16[16,128,128]{2,1,0:T(8,128)(2,1)}), bf16[16,128,128]{2,1,0:T(8,128)(2,1)S(1)}, u32[]{:S(2)}, u32[]{:S(2)}) async-start(bf16[16,128,128]{2,1,0:T(8,128)(2,1)} %shard_map.58), calls=%async_computation | async-start | bytes 1048576 | tf_op jit(solution)/shard_map/all_to_all | solution.py:267
  26.6 3.4 %collective-permute-start.6 = (bf16[4,2,128,128]{3,2,1,0:T(8,128)(2,1)S(1)}, bf16[4,2,128,128]{3,2,1,0:T(8,128)(2,1)S(1)}, u32[]{:S(2)}, u32[]{:S(2)}) collective-permute-start(bf16[4,2,128,128]{3,2,1,0:T(8,128)(2,1)S(1)} %shard_map.56.refs_0_), channel_id=1, source_target_pairs={{0,32},{32,0},{1,33},{33,1},{2,34},{34,2},{3,35},{35,3},{4,36},{36... | collective-permute-start | bytes 786440 | tf_op jit(solution)/shard_map/ppermute | solution.py:276
  27.6 2.5 %collective-permute-start.7 = (bf16[4,2,128,128]{3,2,1,0:T(8,128)(2,1)S(1)}, bf16[4,2,128,128]{3,2,1,0:T(8,128)(2,1)S(1)}, u32[]{:S(2)}, u32[]{:S(2)}) collective-permute-start(bf16[4,2,128,128]{3,2,1,0:T(8,128)(2,1)S(1)} %collective-permute-done.4.refs_1_), channel_id=1, source_target_pairs={{0,32},{32,0},{1,33},{33,1},{2,34},{34,2},{3,35},{35,3},{4,36},{36... | collective-permute-start | bytes 786440 | tf_op jit(solution)/shard_map/ppermute | solution.py:276
  29.7 1.6 %collective-permute-start.8 = (bf16[4,2,128,128]{3,2,1,0:T(8,128)(2,1)S(1)}, bf16[4,2,128,128]{3,2,1,0:T(8,128)(2,1)S(1)}, u32[]{:S(2)}, u32[]{:S(2)}) collective-permute-start(bf16[4,2,128,128]{3,2,1,0:T(8,128)(2,1)S(1)} %collective-permute-done.5.refs_2_), channel_id=1, source_target_pairs={{0,32},{32,0},{1,33},{33,1},{2,34},{34,2},{3,35},{35,3},{4,36},{36... | collective-permute-start | bytes 786440 | tf_op jit(solution)/shard_map/ppermute | solution.py:276
  55.0 8.8 %collective-permute-start.9 = (bf16[128,512]{1,0:T(8,128)(2,1)S(1)}, bf16[128,512]{1,0:T(8,128)(2,1)S(1)}, u32[]{:S(2)}, u32[]{:S(2)}) collective-permute-start(bf16[128,512]{1,0:T(8,128)(2,1)S(1)} %shard_map.61), channel_id=1, source_target_pairs={{248,0},{249,1},{250,2},{251,3},{88,4},{89,5},{90,6},{91,7},{24,8}... | collective-permute-start | bytes 393224 | tf_op jit(solution)/shard_map/ppermute | solution.py:347
